TPU v7x, 128 devices: a whole 4x4x4 slice. The times are simulated.
128 devices in a mesh: row: 8 (over y, core), col: 16 (over z, x).
Axes of the slice: x: 4, y: 4, z: 4, core: 2. Of those that a mesh axis runs over, the one named last changes fastest.
Arguments:
- ancestor_inverse: float32 [12288, 12288], P('row', 'col')
- factor: bfloat16 [3, 12288, 512], P(None, ('row', 'col')), may hold values from -0.5 to 0.5
- coupling: float32 [3, 512, 512], replicated, may hold values from -0.25 to 0.25
- diagonal_inverse: float32 [3, 512, 512], replicated, may hold values from -6 to 6
- ancestors: int32 [3, 24], replicated, may hold values from -1 to 23, as said below
Outputs:
- block_columns: float32 [3, 12288, 512], P(None, ('row', 'col'))
- block_rows: float32 [3, 12288, 512], P(None, ('col', 'row'))
- node_blocks: float32 [3, 3, 512, 512], replicated
Inputs may be any that keep to these rules, and one draw needn't show every extreme that they name: `ancestors`: row k lists the ancestor block rows of supernode k, blocks of 512 rows: distinct indices in increasing order, then -1 in the slots left. Every block is listed by some supernode.
All inputs are finite; a program needn't handle non-finite values.
Results may differ from a plain program's by a relative error of at most 0.0003.
Values may be sent and summed in bfloat16 or wider, within the bound.
A program may use at most 128 MiB of HBM per device.

v0:
```python
import jax
import jax.numpy as jnp
from jax import lax
from jax.sharding import PartitionSpec as P

highest = lax.Precision.HIGHEST


def broadcast(value, axis, source):
    kept = jnp.where(lax.axis_index(axis) == source, value, 0).astype(value.dtype)
    return lax.psum(kept, axis)


def matmul(left, right):
    return jnp.dot(left, right, precision=highest)


def left_dot(left, right):
    return lax.dot_general(left, right, (((0,), (0,)), ((), ())), precision=highest)


def pair_index(later, earlier):
    return later * (later - 1) // 2 + earlier


def local(ancestor_inverse, factor, coupling, diagonal_inverse, ancestors):
    col_count = lax.axis_size("col")
    row_count = lax.axis_size("row")
    row_index = lax.axis_index("row")
    col_index = lax.axis_index("col")
    nodes_total, piece_rows, sn_width = factor.shape
    rows_here, cols_here = ancestor_inverse.shape
    group_ratio = rows_here // cols_here
    first_row = (row_index * col_count + col_index) * piece_rows
    block_of_row = (first_row + jnp.arange(piece_rows, dtype=jnp.int32)) // sn_width
    source_row = col_index // group_ratio
    block_start = col_index % group_ratio * cols_here
    row_layout = []
    solved = {}
    for current in range(nodes_total):
        listed = jnp.any(ancestors[current][:, None] == block_of_row[None, :], axis=0)
        lower_part = jnp.where(listed[:, None], factor[current], jnp.zeros_like(factor[current]))
        lower_rows = lax.all_gather(lower_part, "col", axis=0, tiled=True)
        own_block = lax.dynamic_slice_in_dim(lower_rows, block_start, cols_here, 0)
        lower_cols = broadcast(own_block, "row", source_row).astype(jnp.float32)
        lower_here = lower_part.astype(jnp.float32)
        product_sum = lax.psum_scatter(
            matmul(ancestor_inverse, lower_cols), "col", scatter_dimension=0, tiled=True
        )
        for earlier in range(current):
            product_sum = product_sum + matmul(
                row_layout[earlier], coupling[pair_index(current, earlier)]
            )
        column = -product_sum
        stacked = jnp.concatenate(row_layout + [column], axis=1)
        summed = lax.psum(left_dot(lower_here, stacked), ("row", "col"))
        crosses = [
            summed[:, earlier * sn_width : (earlier + 1) * sn_width] for earlier in range(current)
        ]
        self_term = summed[:, current * sn_width : (current + 1) * sn_width]
        for earlier in range(current):
            block_value = -crosses[earlier].T
            for inner in range(current):
                block_value = block_value - matmul(
                    solved[earlier, inner], coupling[pair_index(current, inner)]
                )
            solved[earlier, current] = block_value
            solved[current, earlier] = block_value.T
        diag_value = diagonal_inverse[current] - self_term
        for earlier in range(current):
            diag_value = diag_value - left_dot(
                coupling[pair_index(current, earlier)], solved[earlier, current]
            )
        solved[current, current] = diag_value
        row_layout.append(column)
    finished = jnp.stack(row_layout)
    part_rows = piece_rows // row_count
    ratio_cols = col_count // row_count
    split_parts = finished.reshape(nodes_total, row_count, part_rows, sn_width)
    held = lax.all_to_all(split_parts, "row", split_axis=1, concat_axis=1, tiled=True)
    targets = jnp.arange(row_count, dtype=jnp.int32) * ratio_cols + col_index // row_count
    onehot = (targets[:, None] == jnp.arange(col_count, dtype=jnp.int32)[None, :]).astype(
        jnp.float32
    )
    slotted = jnp.einsum("rc,nrqs->ncqs", onehot, held, precision=highest)
    arrived = lax.all_to_all(slotted, "col", split_axis=1, concat_axis=1, tiled=True)
    picked = lax.dynamic_slice_in_dim(arrived, col_index % ratio_cols * row_count, row_count, 1)
    landed = lax.all_to_all(picked, "row", split_axis=1, concat_axis=1, tiled=True)
    mirrored_all = landed.reshape(nodes_total, piece_rows, sn_width)
    node_blocks = jnp.stack(
        [
            jnp.stack([solved[first_node, second_node] for second_node in range(nodes_total)])
            for first_node in range(nodes_total)
        ]
    )
    return (finished, mirrored_all, node_blocks)


def solution(mesh):
    placed = (P("row", "col"), P(None, ("row", "col"), None), P(), P(), P())
    return jax.shard_map(
        local,
        mesh=mesh,
        in_specs=placed,
        out_specs=(P(None, ("row", "col"), None), P(None, ("col", "row"), None), P()),
        check_vma=False,
    )
```

profile of v0, /device:TPU:1, one launch (start us, length us, event | category | flops | bytes accessed | tf_op | source)
XLA Modules:
  0.0 691.0 jit_solution(10552824575240240170)
XLA Ops:
  11.5 45.6 %all-gather.6.cloned.1.call-done = bf16[1536,512]{1,0:T(8,128)(2,1)} async-done(((bf16[96,512]{1,0:T(8,128)(2,1)}), bf16[1536,512]{1,0:T(8,128)(2,1)}) %all-gather.6.cloned.1.call-update) | async-done | bytes 1572880 | tf_op jit(solution)/shard_map/all_gather | solution.py:43
  57.1 2.2 dynamic-slice_select_fusion.1
  59.2 43.3 %all-gather.4.cloned.1.call-done = bf16[1536,512]{1,0:T(8,128)(2,1)} async-done(((bf16[96,512]{1,0:T(8,128)(2,1)}), bf16[1536,512]{1,0:T(8,128)(2,1)}) %all-gather.4.cloned.1.call-update) | async-done | bytes 1572880 | tf_op jit(solution)/shard_map/all_gather | solution.py:43
  102.5 2.1 dynamic-slice_select_fusion.2
  104.7 43.3 %all-gather.8.cloned.1.call-done = bf16[1536,512]{1,0:T(8,128)(2,1)} async-done(((bf16[96,512]{1,0:T(8,128)(2,1)}), bf16[1536,512]{1,0:T(8,128)(2,1)}) %all-gather.8.cloned.1.call-update) | async-done | bytes 1572880 | tf_op jit(solution)/shard_map/all_gather | solution.py:43
  148.0 2.1 dynamic-slice_select_fusion
  150.3 66.0 %all-reduce.7.cloned.1.call-done = (bf16[768,512]{1,0:T(8,128)(2,1)}, bf16[768,512]{1,0:T(8,128)(2,1)}, bf16[768,512]{1,0:T(8,128)(2,1)}) async-done(((bf16[768,512]{1,0:T(8,128)(2,1)}, bf16[768,512]{1,0:T(8,128)(2,1)}, bf16[768,512]{1,0:T(8,128)(2,1)}), (bf16[768,512]{1,0:T(8,128)(2,1)}, bf16[768,512]{1,0:T(8,128)(2,1)}, bf16[768,512]{1,0:T(8,128)(2,1)})) %all-reduce.7.cloned.1.call-update) | async-done | bytes 2359312 | tf_op jit(solution)/shard_map/psum | solution.py:11
  216.2 6.7 convolution_bitcast_fusion.2
  222.9 2.3 copy.104
  225.3 6.7 convolution_bitcast_fusion.1
  232.0 2.4 copy.106
  234.5 6.7 convolution_bitcast_fusion
  241.2 2.4 copy.108
  244.1 57.1 %reduce-scatter.10.cloned.1.call-done = f32[96,512]{1,0:T(8,128)} async-done(((f32[1536,512]{1,0:T(8,128)}), f32[96,512]{1,0:T(8,128)}) %reduce-scatter.10.cloned.1.call-update) | async-done | bytes 196624 | tf_op jit(solution)/shard_map/reduce_scatter | solution.py:47
  301.2 78.3 %reduce-scatter.12.cloned.1.call-done = f32[96,512]{1,0:T(8,128)} async-done(((f32[1536,512]{1,0:T(8,128)}), f32[96,512]{1,0:T(8,128)}) %reduce-scatter.12.cloned.1.call-update) | async-done | bytes 196624 | tf_op jit(solution)/shard_map/reduce_scatter | solution.py:47
  381.3 77.3 %reduce-scatter.14.cloned.1.call-done = f32[96,512]{1,0:T(8,128)} async-done(((f32[1536,512]{1,0:T(8,128)}), f32[96,512]{1,0:T(8,128)}) %reduce-scatter.14.cloned.1.call-update) | async-done | bytes 196624 | tf_op jit(solution)/shard_map/reduce_scatter | solution.py:47
  458.6 1.8 convolution_add_fusion.1
  461.9 2.3 fusion.45
  464.2 3.1 fusion.38
  475.2 6.7 all-to-all-start
  481.9 15.6 %all-to-all-done = f32[3,8,12,512]{3,2,0,1:T(8,128)} async-done(((f32[3,8,12,512]{3,2,0,1:T(8,128)}), f32[3,8,12,512]{3,2,0,1:T(8,128)}, u32[]{:S(2)}, u32[]{:S(2)}) %all-to-all-start) | async-done | bytes 589856 | tf_op jit(solution)/shard_map/all_to_all | solution.py:80
  497.5 2.1 convolution_bitcast_fusion.3
  499.6 1.9 copy.80
  501.5 4.8 all-to-all-start.1
  506.3 21.0 %all-to-all-done.1 = f32[3,16,12,512]{3,2,0,1:T(8,128)} async-done(((f32[3,16,12,512]{3,2,0,1:T(8,128)}), f32[3,16,12,512]{3,2,0,1:T(8,128)}, u32[]{:S(2)}, u32[]{:S(2)}) %all-to-all-start.1) | async-done | bytes 1179680 | tf_op jit(solution)/shard_map/all_to_all | solution.py:86
  527.3 2.1 constant_dynamic-slice_fusion
  529.4 9.0 %all-to-all-start.2 = ((f32[3,8,12,512]{3,2,0,1:T(8,128)}), f32[3,8,12,512]{3,2,0,1:T(8,128)}, u32[]{:S(2)}, u32[]{:S(2)}) async-start(f32[3,8,12,512]{3,2,0,1:T(8,128)} %constant_dynamic-slice_fusion), calls=%async_computation.2 | async-start | bytes 1572864 | tf_op jit(solution)/shard_map/all_to_all | solution.py:88
  538.4 2.4 slice.71
  540.8 2.6 copy.110
  543.4 1.8 pad_maximum_fusion.2
  545.1 5.7 all-to-all-done.2
  550.9 2.2 copy.81
  553.0 2.0 reshape.46
  555.1 83.9 %all-reduce.5.cloned.1.call-done = (f32[512,1536]{1,0:T(8,128)}, f32[512,512]{1,0:T(8,128)}, f32[512,1024]{0,1:T(8,128)}) async-done(((f32[512,1536]{1,0:T(8,128)}, f32[512,512]{1,0:T(8,128)}, f32[512,1024]{0,1:T(8,128)}), (f32[512,1536]{1,0:T(8,128)}, f32[512,512]{1,0:T(8,128)}, f32[512,1024]{0,1:T(8,128)})) %all-reduce.5.cloned.1.call-update) | async-done | bytes 6291472 | tf_op jit(solution)/shard_map/psum | solution.py:56
  638.9 3.8 bitcast_subtract_fusion.7
  642.7 1.9 fusion.14
  644.6 1.9 fusion.18
  646.6 1.9 fusion.20
  648.5 2.0 fusion.3
  651.5 2.1 fusion.12
  653.7 3.1 fusion.2
  656.8 2.3 fusion.7
  659.1 2.3 fusion.60
  661.4 2.6 copy.85
  663.9 3.8 maximum_bitcast_fusion.1
  667.8 3.6 copy.95
  671.3 4.3 fusion.1
  679.1 4.9 pad_maximum_fusion
  (78 shorter events, 20.5 us)
Async XLA Ops:
  7.2 49.9 %all-gather.6.cloned.1.call-start = ((), (), s32[]{:S(2)}) async-start(), calls=%async_computation.7 | async-start | bytes 1671168 | tf_op jit(solution)/shard_map/all_gather | solution.py:43
  9.9 92.6 %all-gather.4.cloned.1.call-start = ((), (), s32[]{:S(2)}) async-start(), calls=%async_computation.6 | async-start | bytes 1671168 | tf_op jit(solution)/shard_map/all_gather | solution.py:43
  10.7 137.4 %all-gather.8.cloned.1.call-start = ((), (), s32[]{:S(2)}) async-start(), calls=%async_computation.8 | async-start | bytes 1671168 | tf_op jit(solution)/shard_map/all_gather | solution.py:43
  11.4 204.8 %all-reduce.7.cloned.1.call-start = ((), (), s32[]{:S(2)}) async-start(), calls=%async_computation.13 | async-start | bytes 4718592 | tf_op jit(solution)/shard_map/psum | solution.py:11
  150.2 151.0 %reduce-scatter.10.cloned.1.call-start = ((), (), s32[]{:S(2)}) async-start(), calls=%async_computation.9 | async-start | bytes 3342336 | tf_op jit(solution)/shard_map/reduce_scatter | solution.py:47
  225.3 154.3 %reduce-scatter.12.cloned.1.call-start = ((), (), s32[]{:S(2)}) async-start(), calls=%async_computation.10 | async-start | bytes 3342336 | tf_op jit(solution)/shard_map/reduce_scatter | solution.py:47
  234.4 224.1 %reduce-scatter.14.cloned.1.call-start = ((), (), s32[]{:S(2)}) async-start(), calls=%async_computation.11 | async-start | bytes 3342336 | tf_op jit(solution)/shard_map/reduce_scatter | solution.py:47
  243.6 136.0 %copy-start = (f32[3,512,512]{2,1,0:T(8,128)S(1)}, f32[3,512,512]{2,1,0:T(8,128)}, u32[]{:S(2)}) copy-start(f32[3,512,512]{2,1,0:T(8,128)} %param.7) | copy-start | bytes 9437188
  243.6 395.3 %all-reduce.5.cloned.1.call-start = ((), (), s32[]{:S(2)}) async-start(), calls=%async_computation.12 | async-start | bytes 12582912 | tf_op jit(solution)/shard_map/psum | solution.py:56
  301.2 159.9 %copy-start.16 = (f32[96,512]{1,0:T(8,128)S(1)}, f32[96,512]{1,0:T(8,128)}, u32[]{:S(2)}) copy-start(f32[96,512]{1,0:T(8,128)} %reduce-scatter.10.cloned.1.call-done) | copy-start | bytes 589828
  458.6 3.3 copy-start.20
  458.6 5.7 copy-start.22
  461.1 6.2 copy-start.17
  461.9 5.5 copy-start.19
  461.9 5.5 copy-start.21
  469.0 0.9 copy-start.18
  475.2 22.3 %all-to-all-start = ((f32[3,8,12,512]{3,2,0,1:T(8,128)}), f32[3,8,12,512]{3,2,0,1:T(8,128)}, u32[]{:S(2)}, u32[]{:S(2)}) async-start(f32[3,8,12,512]{3,2,0,1:T(8,128)} %copy.78), calls=%async_computation | async-start | bytes 1572864 | tf_op jit(solution)/shard_map/all_to_all | solution.py:80
  501.5 25.8 %all-to-all-start.1 = ((f32[3,16,12,512]{3,2,0,1:T(8,128)}), f32[3,16,12,512]{3,2,0,1:T(8,128)}, u32[]{:S(2)}, u32[]{:S(2)}) async-start(f32[3,16,12,512]{3,2,0,1:T(8,128)} %copy.80), calls=%async_computation.1 | async-start | bytes 3145728 | tf_op jit(solution)/shard_map/all_to_all | solution.py:86
  529.4 21.4 %all-to-all-start.2 = ((f32[3,8,12,512]{3,2,0,1:T(8,128)}), f32[3,8,12,512]{3,2,0,1:T(8,128)}, u32[]{:S(2)}, u32[]{:S(2)}) async-start(f32[3,8,12,512]{3,2,0,1:T(8,128)} %constant_dynamic-slice_fusion), calls=%async_computation.2 | async-start | bytes 1572864 | tf_op jit(solution)/shard_map/all_to_all | solution.py:88
  642.7 5.8 copy-start.1
  642.7 3.8 copy-start.8
  642.7 3.8 copy-start.9
  644.6 3.9 copy-start.10
  644.6 3.9 copy-start.11
  646.6 12.5 %copy-start.3 = (f32[512,512]{0,1:T(8,128)}, f32[512,512]{0,1:T(8,128)S(1)}, u32[]{:S(2)}) copy-start(f32[512,512]{0,1:T(8,128)S(1)} %fusion.18) | copy-start | bytes 3145732
  648.5 5.1 copy-start.6
  650.5 1.0 copy-start.7
  653.7 5.4 copy-start.4
  671.3 4.3 copy-start.2
  671.3 4.3 copy-start.12
  671.3 4.3 copy-start.15
  675.7 1.2 copy-start.13
  675.7 1.5 copy-start.14
  677.2 1.9 copy-start.5
Sparse Core Ops, SparseCore 0:
  10.7 46.3 all-gather.5
  59.2 43.3 all-gather.3
  104.7 43.3 all-gather.7
  151.0 65.1 all-reduce.6
  225.4 75.7 reduce-scatter.9
  304.4 75.1 reduce-scatter.11
  383.4 75.0 reduce-scatter.13
  469.1 169.7 all-reduce.4
where the time goes:
time: 699 us; the launch traced here: 691 us
  waiting for transfers between devices  539 us (77%)
  matrix products  54.5 us (8%)
  local copies, waits for them, and re-layouts  36 us (5%)
  other arithmetic  26 us (4%)
  starting transfers between devices  21.2 us (3%)
  between operations  14.7 us (2%)
    reduce_scatter x3, waiting for transfers between devices, local(): lax.psum_scatter(matmul(ancestor_inverse, lower_cols), 'col', scatter_dim...  213 us
    all_gather x3, waiting for transfers between devices, local(): lower_rows = lax.all_gather(lower_part, 'col', axis=0, tiled=True)  132 us
    psum x1, waiting for transfers between devices, local(): summed = lax.psum(left_dot(lower_here, stacked), ('row', 'col'))  83.9 us
    psum x1, waiting for transfers between devices, broadcast(): return lax.psum(kept, axis)  66 us
    dot_general x11, matrix products, matmul(): return jnp.dot(left, right, precision=highest)  36 us
    all_to_all x1, waiting for transfers between devices, local(): lax.all_to_all(slotted, 'col', split_axis=1, concat_axis=1, tiled=True)  21 us
    dot_general x6, matrix products, left_dot(): lax.dot_general(left, right, (((0,), (0,)), ((), ())), precision=highest)  16.5 us
    all_to_all x1, waiting for transfers between devices, local(): lax.all_to_all(split_parts, 'row', split_axis=1, concat_axis=1, tiled=True)  15.6 us
  transfers between devices with their start and end apart: 11, of which 11 were waited for; matrix products, arithmetic and copies ran while one was open for 7% of the time, Pallas kernels for 0%

commit v1 on v0

v1 whole, which is shorter than its diff:
```python
import jax
import jax.numpy as jnp
from jax import lax
from jax.experimental import pallas as pl
from jax.experimental.pallas import tpu as pltpu
from jax.sharding import PartitionSpec as P

MESH = pl.DeviceIdType.MESH
F32 = jnp.float32
BF16 = jnp.bfloat16
NODES = 3
SN = 512
HALF = 256
PIECE = 96
ROWS = 1536
COLS = 768
PAIRS = ((0, 0), (0, 1), (1, 1), (0, 2), (1, 2), (2, 2))


def pair_index(later, earlier):
    return later * (later - 1) // 2 + earlier


def split(value):
    high = value.astype(BF16)
    return high, (value - high.astype(F32)).astype(BF16)


def dot(left, right):
    return jnp.dot(left, right, preferred_element_type=F32)


def dot3(left, right_high, right_low):
    high, low = split(left)
    return dot(high, right_high) + dot(high, right_low) + dot(low, right_high)


def kernel(
    inverse, factor, coupling, diagonal, ancestors,
    rows_out, columns_out, upper_out,
    inv, inv_high, inv_low, own_masked, lower, partial, traded, arrived,
    couple, couple_high, couple_low, diag, tail, side, side_high, side_low,
    own_lower, tilde, tilde_other, tilde_high, tilde_low, rows_other,
    inner, recv1, recv2, recv3, part1, part2,
    local_sem, gather_send, gather_recv, lower_sem, columns_sem, trade_sem, sum_send, sum_recv,
    tilde_sem, other_sem, down_send, down_recv, up_send, up_recv, swap_sem,
):
    row = lax.axis_index("row")
    col = lax.axis_index("col")
    y, core, z, x = row // 2, row % 2, col // 4, col % 4

    def device(dy=0, dcore=0, dz=0, dx=0):
        return (
            ((y + dy) % 4) * 2 + (core + dcore) % 2,
            ((z + dz) % 4) * 4 + (x + dx) % 4,
        )

    def along(axis, step):
        return device(**{"d" + axis: step % 4})

    coordinate = {"x": x, "y": y, "z": z}
    partner = device(dcore=1)
    forward = (col // 2, (col % 2) * 8 + row)
    backward = (col % 8, 2 * row + col // 8)
    moves = jnp.logical_or(forward[0] != row, forward[1] != col)

    sent = []

    def remote(src, dst, send_sem, recv_sem, target):
        return pltpu.make_async_remote_copy(
            src_ref=src, dst_ref=dst, send_sem=send_sem, recv_sem=recv_sem,
            device_id=target, device_id_type=MESH,
        )

    def start(src, dst, send_sem, recv_sem, target):
        copy = remote(src, dst, send_sem, recv_sem, target)
        copy.start()
        sent.append(copy)
        return copy

    barrier = pltpu.get_barrier_semaphore()
    neighbours = [along(a, s) for a in "xyz" for s in (1, 2, 3)] + [partner]
    for target in neighbours:
        pl.semaphore_signal(barrier, inc=1, device_id=target, device_id_type=MESH)

    @pl.when(moves)
    def _():
        for target in (forward, backward):
            pl.semaphore_signal(barrier, inc=1, device_id=target, device_id_type=MESH)

    load_inv = pltpu.make_async_copy(inverse, inv, local_sem.at[0])
    load_couple = pltpu.make_async_copy(coupling, couple, local_sem.at[1])
    load_diag = pltpu.make_async_copy(diagonal, diag, local_sem.at[2])
    load_inv.start()
    load_couple.start()
    load_diag.start()

    first_row = (row * 16 + col) * PIECE
    first_block = first_row // SN
    last_block = (first_row + PIECE - 1) // SN
    row_at = first_row + lax.broadcasted_iota(jnp.int32, (PIECE, SN), 0)
    in_first = row_at < (first_block + 1) * SN
    for node in range(NODES):
        first_listed = jnp.float32(0)
        last_listed = jnp.float32(0)
        for slot in range(24):
            entry = ancestors[node, slot]
            first_listed = jnp.where(entry == first_block, 1.0, first_listed)
            last_listed = jnp.where(entry == last_block, 1.0, last_listed)
        keep = jnp.where(in_first, first_listed, last_listed)
        masked = jnp.where(keep > 0.5, factor[node].astype(F32), 0.0).astype(BF16)
        own_masked[node] = masked
        lower[node, 0, z, x] = masked[:, :HALF]
        lower[node, 1, z, x] = masked[:, HALF:]

    pl.semaphore_wait(barrier, len(neighbours) + 2 * jnp.where(moves, 1, 0))

    def piece(node, half, first, second):
        return lower.at[node, half, second, first] if half == 0 else lower.at[node, half, first, second]

    def line(node, half, second):
        return lower.at[node, half, second] if half == 0 else lower.at[node, half, :, second]

    def line_part(node, half, second, part):
        where = pl.ds(2 * part, 2)
        return lower.at[node, half, second, where] if half == 0 else lower.at[node, half, where, second]

    axes = ("xz", "zx")

    def gather_copy(node, half, index, ref, axis, step):
        return start(
            ref, ref, gather_send.at[node, half, index], gather_recv.at[node, half, index], along(axis, step)
        )

    copies = {}

    def first_phase(node):
        for half in range(2):
            a = axes[half][0]
            own = piece(node, half, coordinate[a], coordinate[axes[half][1]])
            copies[node, half, 0] = gather_copy(node, half, 0, own, a, 1)
            copies[node, half, 1] = gather_copy(node, half, 1, own, a, 3)

    def first_forward(node):
        for half in range(2):
            a, b = axes[half]
            for index, shift, step, cut in ((0, 3, 1, 0), (1, 1, 3, 128)):
                copies[node, half, index].wait_recv()
                got = piece(node, half, (coordinate[a] + shift) % 4, coordinate[b])
                copies[node, half, index + 2] = gather_copy(
                    node, half, index + 2, got.at[:, pl.ds(cut, 128)], a, step
                )

    def second_phase(node):
        for half in range(2):
            b = axes[half][1]
            copies[node, half, 2].wait_recv()
            copies[node, half, 3].wait_recv()
            own = line(node, half, coordinate[b])
            copies[node, half, 4] = gather_copy(node, half, 4, own, b, 1)
            copies[node, half, 5] = gather_copy(node, half, 5, own, b, 3)

    def second_forward(node):
        for half in range(2):
            b = axes[half][1]
            for index, shift, step, part in ((4, 3, 1, 0), (5, 1, 3, 1)):
                copies[node, half, index].wait_recv()
                got = line_part(node, half, (coordinate[b] + shift) % 4, part)
                copies[node, half, index + 2] = gather_copy(node, half, index + 2, got, b, step)

    def gathered(node, half):
        copies[node, half, 6].wait_recv()
        copies[node, half, 7].wait_recv()

    def multiply(node):
        for half in range(2):
            gathered(node, half)
            right = lower[node, half].reshape(ROWS, HALF)
            for part in range(4):
                rows = pl.ds(part * 192, 192)
                product = dot(inv_high[rows, :], right) + dot(inv_low[rows, :], right)
                partial[node, part, :, :, half * HALF : (half + 1) * HALF] = product.reshape(2, PIECE, HALF)
        copies["trade", node] = start(
            partial.at[node, :, 1 - core], traded.at[node], trade_sem.at[node, 0], trade_sem.at[node, 1], partner
        )

    def reduce_start(node):
        copies["trade", node].wait_recv()
        traded[node] = traded[node] + partial[node, :, core]
        for step in (1, 2, 3):
            copies["sum", node, step] = start(
                traded.at[node, (y + step) % 4], arrived.at[node, step - 1],
                sum_send.at[node, step - 1], sum_recv.at[node, step - 1], along("y", step),
            )

    def permute_copy(node, src, dst, sems, target):
        return remote(src.at[node], dst.at[node], sems.at[node, 0], sems.at[node, 1], target)

    def permute_start(node, src, dst, sems, target):
        @pl.when(moves)
        def _():
            permute_copy(node, src, dst, sems, target).start()

        @pl.when(jnp.logical_not(moves))
        def _():
            dst[node] = src[node]

    def permute_wait(node, src, dst, sems, target):
        @pl.when(moves)
        def _():
            permute_copy(node, src, dst, sems, target).wait()

    def solve(node):
        total = traded[node, y]
        for step in (1, 2, 3):
            copies["sum", node, step].wait_recv()
            total = total + arrived[node, step - 1]
        for earlier in range(node):
            g = pair_index(node, earlier)
            total = total + dot3(rows_out[earlier], couple_high[g], couple_low[g])
        rows_out[node] = -total
        permute_start(node, rows_out, columns_out, columns_sem, forward)
        copies["other", node] = start(
            rows_out.at[node], rows_other.at[node], other_sem.at[node, 0], other_sem.at[node, 1], partner
        )

    def prepare_tilde():
        for node in range(NODES):
            permute_wait(node, own_masked, own_lower, lower_sem, backward)
        for node in range(NODES):
            value = own_lower[node].astype(F32)
            for earlier in range(node):
                g = pair_index(node, earlier)
                value = value - dot3(tilde[earlier], couple_high[g], couple_low[g])
            tilde[node] = value
        copies["tilde"] = start(
            tilde.at[:, :, pl.ds(pl.multiple_of((1 - core) * HALF, HALF), HALF)], tilde_other,
            tilde_sem.at[0], tilde_sem.at[1], partner,
        )

    def transpose_tilde():
        copies["tilde"].wait_recv()
        mine = pl.ds(pl.multiple_of(core * HALF, HALF), HALF)
        for node in range(NODES):
            both = jnp.concatenate([tilde[node, :, mine], tilde_other[node]], axis=0)
            high, low = split(both.T)
            tilde_high[node] = high
            tilde_low[node] = low

    def inner_products(pairs):
        for index in pairs:
            earlier, later = PAIRS[index]
            both = jnp.concatenate([rows_out[later], rows_other[later]], axis=0)
            high, low = split(both)
            value = (
                dot(tilde_high[earlier], high) + dot(tilde_high[earlier], low) + dot(tilde_low[earlier], high)
            )
            inner[index // 2, pl.ds(index % 2 * HALF, HALF), :] = -value

    orders = ("xyz", "yzx", "zxy")
    extents = (128, 32, 8)

    def down_start(part, level, source):
        axis = orders[part][level]
        rows = extents[level]
        land = (recv1, recv2, recv3)[level]
        for step in (1, 2, 3):
            at = pl.multiple_of((coordinate[axis] + step) % 4 * rows, rows)
            copies["down", part, level, step] = start(
                source.at[pl.ds(at, rows)], land.at[part, step - 1],
                down_send.at[part, level, step - 1], down_recv.at[part, level, step - 1], along(axis, step),
            )

    def down_finish(part, level, source):
        axis = orders[part][level]
        rows = extents[level]
        land = (recv1, recv2, recv3)[level]
        total = source[pl.ds(pl.multiple_of(coordinate[axis] * rows, rows), rows), :]
        for step in (1, 2, 3):
            copies["down", part, level, step].wait_recv()
            total = total + land[part, step - 1]
        return total

    def offset(part, levels):
        at = 0
        for level in range(levels):
            at = at + coordinate[orders[part][level]] * extents[level]
        return at

    def up_start(part, level):
        axis = orders[part][level]
        rows = extents[level]
        at = pl.multiple_of(offset(part, level + 1), rows)
        ref = upper_out.at[core, part, pl.ds(at, rows)]
        for step in (1, 2, 3):
            copies["up", part, level, step] = start(
                ref, ref, up_send.at[part, level, step - 1], up_recv.at[part, level, step - 1], along(axis, step)
            )

    def up_wait(part, level):
        for step in (1, 2, 3):
            copies["up", part, level, step].wait_recv()

    def swap(part):
        ref = upper_out.at[core, part]
        copies["swap", part] = start(ref, ref, swap_sem.at[part, 0], swap_sem.at[part, 1], partner)

    def split_side(value):
        high, low = split(value)
        side_high[...] = high
        side_low[...] = low

    def add_product(target, left, high, low, base):
        def body(block, carry):
            rows = pl.ds(pl.multiple_of(block * 128, 128), 128)
            target[rows, :] = base[rows, :] - dot3(left[rows, :], high[...], low[...])
            return carry

        lax.fori_loop(0, 4, body, 0)

    def negate_product(target, left, high, low):
        def body(block, carry):
            rows = pl.ds(pl.multiple_of(block * 128, 128), 128)
            target[rows, :] = -dot3(left[rows, :], high[...], low[...])
            return carry

        lax.fori_loop(0, 4, body, 0)

    e00, e01, e11, e02, e12, e22 = (tail.at[i] for i in range(6))

    def tail_first():
        e00[...] = diag[0]
        negate_product(e01, diag.at[0], couple_high.at[0], couple_low.at[0])
        negate_product(e02, diag.at[0], couple_high.at[1], couple_low.at[1])
        add_product(e02, e01, couple_high.at[2], couple_low.at[2], e02)

    def tail_second():
        split_side(e01[...])
        side[...] = couple[0].T
        add_product(e11, side, side_high, side_low, diag.at[1])
        side[...] = e01[...].T
        negate_product(e12, side, couple_high.at[1], couple_low.at[1])
        add_product(e12, e11, couple_high.at[2], couple_low.at[2], e12)

    def tail_third():
        split_side(e02[...])
        side[...] = couple[1].T
        add_product(e22, side, side_high, side_low, diag.at[2])
        split_side(e12[...])
        side[...] = couple[2].T
        add_product(e22, side, side_high, side_low, e22)

    for node in range(NODES):
        first_phase(node)
        permute_start(node, own_masked, own_lower, lower_sem, backward)
    load_inv.wait()
    first_forward(0)
    second_phase(0)
    first_forward(1)
    first_forward(2)
    for block in range(6):
        where = slice(block * 256, (block + 1) * 256)
        high, low = split(inv[where, :].T)
        inv_high[:, where] = high
        inv_low[:, where] = low
    second_forward(0)
    second_phase(1)
    load_couple.wait()
    load_diag.wait()
    for g in range(3):
        high, low = split(couple[g])
        couple_high[g] = high
        couple_low[g] = low
    multiply(0)
    second_forward(1)
    second_phase(2)
    reduce_start(0)
    tail_first()
    multiply(1)
    second_forward(2)
    reduce_start(1)
    prepare_tilde()
    tail_second()
    solve(0)
    multiply(2)
    reduce_start(2)
    transpose_tilde()
    solve(1)
    tail_third()
    copies["other", 0].wait_recv()
    copies["other", 1].wait_recv()
    inner_products((0, 1, 2))
    down_start(0, 0, inner.at[0])
    solve(2)
    copies["other", 2].wait_recv()
    inner_products((3,))
    down_start(1, 0, inner.at[1])
    inner_products((4, 5))
    down_start(2, 0, inner.at[2])
    for part in range(3):
        part1[part] = down_finish(part, 0, inner.at[part])
        down_start(part, 1, part1.at[part])
    for part in range(3):
        part2[part] = down_finish(part, 1, part1.at[part])
        down_start(part, 2, part2.at[part])
    for part in range(3):
        at = offset(part, 3)
        base = tail[2 * part + at // HALF, pl.ds(pl.multiple_of(core * HALF + at % HALF, 8), 8), :]
        upper_out[core, part, pl.ds(pl.multiple_of(at, 8), 8), :] = base + down_finish(part, 2, part2.at[part])
        up_start(part, 2)
    for level in (1, 0):
        for part in range(3):
            up_wait(part, level + 1)
            up_start(part, level)
    for part in range(3):
        up_wait(part, 0)
        swap(part)
    for part in range(3):
        copies["swap", part].wait_recv()
    for node in range(NODES):
        permute_wait(node, rows_out, columns_out, columns_sem, forward)
    for copy in sent:
        copy.wait_send()


def fused(ancestor_inverse, factor, coupling, diagonal_inverse, ancestors):
    vmem = pl.BlockSpec(memory_space=pltpu.VMEM)
    hbm = pl.BlockSpec(memory_space=pl.ANY)
    dma = pltpu.SemaphoreType.DMA
    square = (SN, SN)
    return pl.pallas_call(
        kernel,
        out_shape=(
            jax.ShapeDtypeStruct((NODES, PIECE, SN), F32),
            jax.ShapeDtypeStruct((NODES, PIECE, SN), F32),
            jax.ShapeDtypeStruct((2, 3, SN, SN), F32),
        ),
        in_specs=[hbm, vmem, hbm, hbm, pl.BlockSpec(memory_space=pltpu.SMEM)],
        out_specs=(vmem, vmem, vmem),
        scratch_shapes=[
            pltpu.VMEM((ROWS, COLS), F32),
            pltpu.VMEM((COLS, ROWS), BF16),
            pltpu.VMEM((COLS, ROWS), BF16),
            pltpu.VMEM((NODES, PIECE, SN), BF16),
            pltpu.VMEM((NODES, 2, 4, 4, PIECE, HALF), BF16),
            pltpu.VMEM((NODES, 4, 2, PIECE, SN), F32),
            pltpu.VMEM((NODES, 4, PIECE, SN), F32),
            pltpu.VMEM((NODES, 3, PIECE, SN), F32),
            pltpu.VMEM((3,) + square, F32),
            pltpu.VMEM((3,) + square, BF16),
            pltpu.VMEM((3,) + square, BF16),
            pltpu.VMEM((3,) + square, F32),
            pltpu.VMEM((6,) + square, F32),
            pltpu.VMEM(square, F32),
            pltpu.VMEM(square, BF16),
            pltpu.VMEM(square, BF16),
            pltpu.VMEM((NODES, PIECE, SN), BF16),
            pltpu.VMEM((NODES, PIECE, SN), F32),
            pltpu.VMEM((NODES, PIECE, HALF), F32),
            pltpu.VMEM((NODES, HALF, 2 * PIECE), BF16),
            pltpu.VMEM((NODES, HALF, 2 * PIECE), BF16),
            pltpu.VMEM((NODES, PIECE, SN), F32),
            pltpu.VMEM((3,) + square, F32),
            pltpu.VMEM((3, 3, 128, SN), F32),
            pltpu.VMEM((3, 3, 32, SN), F32),
            pltpu.VMEM((3, 3, 8, SN), F32),
            pltpu.VMEM((3, 128, SN), F32),
            pltpu.VMEM((3, 32, SN), F32),
            dma((3,)),
            dma((NODES, 2, 8)),
            dma((NODES, 2, 8)),
            dma((NODES, 2)),
            dma((NODES, 2)),
            dma((NODES, 2)),
            dma((NODES, 3)),
            dma((NODES, 3)),
            dma((2,)),
            dma((NODES, 2)),
            dma((3, 3, 3)),
            dma((3, 3, 3)),
            dma((3, 3, 3)),
            dma((3, 3, 3)),
            dma((3, 2)),
        ],
        compiler_params=pltpu.CompilerParams(
            collective_id=0, has_side_effects=True, vmem_limit_bytes=62 << 20
        ),
        name="selected_inversion",
    )(ancestor_inverse, factor, coupling, diagonal_inverse, ancestors)


def local(ancestor_inverse, factor, coupling, diagonal_inverse, ancestors):
    block_rows, block_columns, upper = fused(
        ancestor_inverse, factor, coupling, diagonal_inverse, ancestors
    )
    blocks = {}
    for index, (earlier, later) in enumerate(PAIRS):
        part = upper[:, index // 2, index % 2 * HALF : (index % 2 + 1) * HALF]
        blocks[earlier, later] = part.reshape(SN, SN)
    for earlier, later in PAIRS:
        if earlier != later:
            blocks[later, earlier] = blocks[earlier, later].T
    node_blocks = jnp.stack([jnp.stack([blocks[j, k] for k in range(NODES)]) for j in range(NODES)])
    return block_columns, block_rows, node_blocks


def solution(mesh):
    placed = (P("row", "col"), P(None, ("row", "col"), None), P(), P(), P())
    return jax.shard_map(
        local,
        mesh=mesh,
        in_specs=placed,
        out_specs=(P(None, ("row", "col"), None), P(None, ("col", "row"), None), P()),
        check_vma=False,
    )
```

time: 699 us -> 178 us (0.25)
  waiting for transfers between devices: 539 us -> 0 us
  Pallas kernels: 0 us -> 156 us
  matrix products: 54.5 us -> 0 us
  local copies, waits for them, and re-layouts: 36 us -> 11.2 us
  starting transfers between devices: 21.2 us -> 0 us
  other arithmetic: 26 us -> 8.19 us
  between operations: 14.7 us -> 0.69 us
    reduce_scatter x3 -> x0, waiting for transfers between devices: 213 us -> none  [local(): lax.psum_scatter(matmul(ancestor_inverse, lower_cols), 'col', scatter_dim...]
    pallas_call x0 -> x1, Pallas kernels: none -> 156 us  [fused(): pl.pallas_call(kernel, out_shape=(jax.ShapeDtypeStruct((NODES, PIECE, SN)...]
    psum x2 -> x0, waiting for transfers between devices: 150 us -> none  [the longest x1 83.9 us: local(): summed = lax.psum(left_dot(lower_here, stacked), ('row', 'col'))]
    all_gather x3 -> x0, waiting for transfers between devices: 132 us -> none  [local(): lower_rows = lax.all_gather(lower_part, 'col', axis=0, tiled=True)]
    dot_general x18 -> x0, matrix products: 54.5 us -> none  [the longest x11 36 us: matmul(): return jnp.dot(left, right, precision=highest)]
    all_to_all x3 -> x0, waiting for transfers between devices: 42.3 us -> none  [the longest x1 21 us: local(): lax.all_to_all(slotted, 'col', split_axis=1, concat_axis=1, tiled=True)]
    all_to_all x3 -> x0, starting transfers between devices: 20.4 us -> none  [the longest x1 9.01 us: local(): lax.all_to_all(picked, 'row', split_axis=1, concat_axis=1, tiled=True)]
    unnamed x50 -> x12, local copies, waits for them, and re-layouts: 14.4 us -> 2.1 us
  transfers between devices with their start and end apart: 11 -> 0, of which waited for: 11 -> 0; matrix products, arithmetic and copies ran while one was open for 7% -> 0% of each run, Pallas kernels for 0% -> 0%
where the time goes in v1:
time: 178 us; the launch traced here: 176 us
  Pallas kernels  156 us (88%)
  local copies, waits for them, and re-layouts  11.2 us (6%)
  other arithmetic  8.19 us (5%)
    pallas_call x1, Pallas kernels, fused(): pl.pallas_call(kernel, out_shape=(jax.ShapeDtypeStruct((NODES, PIECE, SN)...  156 us
    another operation x3, other arithmetic, local(): jnp.stack([jnp.stack([blocks[j, k] for k in range(NODES)]) for j in range...  8.19 us
    slice x1, local copies, waits for them, and re-layouts, local(): part = upper[:, index // 2, index % 2 * HALF:(index % 2 + 1) * HALF]  5.09 us
    another operation x3, local copies, waits for them, and re-layouts, local(): blocks[earlier, later] = part.reshape(SN, SN)  3.99 us

profile of v1, /device:TPU:1, one launch (start us, length us, event | category | flops | bytes accessed | tf_op | source)
XLA Modules:
  0.0 176.2 jit_solution(2039803158127052766)
XLA Ops:
  0.6 156.2 %selected_inversion.1 = (f32[3,96,512]{2,1,0:T(8,128)}, f32[3,96,512]{2,1,0:T(8,128)}, f32[2,3,512,512]{3,2,1,0:T(8,128)}) custom-call(f32[1536,768]{1,0:T(8,128)} %inverse.1, bf16[3,96,512]{2,1,0:T(8,128)(2,1)} %factor.1, f32[3,512,512]{2,1,0:T(8,128)} %coupling.1, f32[3,512,512]{2,1,0:T(8,128)} %diagonal.1, s32[3,24]{1,0:T(4,128)} %ancestors.1), custom_call_target="tpu_custom_call" | custom-call | tf_op jit(solution)/shard_map/selected_inversion/pallas_call | solution.py:431
  156.8 5.1 %fusion = (f32[2,1,256,512]{3,2,1,0:T(8,128)}, f32[2,1,256,512]{3,2,1,0:T(8,128)}, f32[2,1,256,512]{3,2,1,0:T(8,128)S(1)}, f32[2,1,256,512]{3,2,1,0:T(8,128)}, f...) fusion(f32[2,3,512,512]{3,2,1,0:T(8,128)} %get-tuple-element.8), kind=kLoop, calls=%fused_computation.4 | loop fusion | bytes 12582912 | tf_op jit(solution)/shard_map/slice | solution.py:498
  161.9 1.3 copy.8
  163.2 1.3 copy.9
  164.5 1.4 copy.10
  165.9 0.0 copy-start
  165.9 0.0 copy-start.1
  165.9 0.0 copy-start.2
  165.9 2.3 %maximum_bitcast_fusion.2 = f32[1,3,512,512]{3,2,1,0:T(8,128)S(1)} fusion(f32[1,512,512]{2,1,0:T(8,128)} %bitcast.33, f32[1,512,512]{2,1,0:T(8,128)} %bitcast.35, f32[1,512,512]{2,1,0:T(8,128)} %bitcast.34), kind=kLoop, calls=%fused_computation.3 | loop fusion | flops 1572864 | bytes 6291456 | tf_op jit(solution)/shard_map/stack | solution.py:503
  168.2 0.0 copy-done
  168.3 0.1 copy-done.1
  168.4 0.3 copy-done.2
  168.7 1.0 maximum_bitcast_fusion
  169.7 0.0 copy-start.4
  169.7 0.0 copy-start.3
  169.7 4.9 %pad_maximum_fusion = f32[3,3,512,512]{3,2,1,0:T(8,128)} fusion(f32[1,3,512,512]{3,2,1,0:T(8,128)S(1)} %maximum_bitcast_fusion.2, f32[1,3,512,512]{3,2,1,0:T(8,128)S(1)} %get-tuple-element.16, f32[1,3,512,512]{3,2,1,0:T(8,128)S(1)} %get-tuple-element.15), kind=kLoop, calls=%fused_computation | loop fusion | flops 4718592 | bytes 18874368 | tf_op jit(solution)/shard_map/stack | solution.py:503
  174.6 0.0 copy-done.4
  174.6 0.8 copy.13
  175.4 0.0 copy-done.3
  175.4 0.8 copy.14
Async XLA Ops:
  165.9 2.3 %copy-start = (f32[2,1,256,512]{3,2,1,0:T(8,128)S(1)}, f32[2,1,256,512]{3,2,1,0:T(8,128)}, u32[]{:S(2)}) copy-start(f32[2,1,256,512]{3,2,1,0:T(8,128)} %get-tuple-element.9) | copy-start | bytes 3145732
  165.9 2.5 %copy-start.1 = (f32[2,1,256,512]{3,2,1,0:T(8,128)S(1)}, f32[2,1,256,512]{3,2,1,0:T(8,128)}, u32[]{:S(2)}) copy-start(f32[2,1,256,512]{3,2,1,0:T(8,128)} %get-tuple-element.12) | copy-start | bytes 3145732
  165.9 2.8 %copy-start.2 = (f32[512,512]{0,1:T(8,128)S(1)}, f32[512,512]{0,1:T(8,128)}, u32[]{:S(2)}) copy-start(f32[512,512]{0,1:T(8,128)} %copy.8) | copy-start | bytes 3145732
  169.7 4.9 %copy-start.4 = (f32[3,96,512]{2,1,0:T(8,128)S(1)}, f32[3,96,512]{2,1,0:T(8,128)}, u32[]{:S(2)}) copy-start(f32[3,96,512]{2,1,0:T(8,128)} %get-tuple-element.20) | copy-start | bytes 1769476
  169.7 5.7 %copy-start.3 = (f32[3,96,512]{2,1,0:T(8,128)S(1)}, f32[3,96,512]{2,1,0:T(8,128)}, u32[]{:S(2)}) copy-start(f32[3,96,512]{2,1,0:T(8,128)} %get-tuple-element.21) | copy-start | bytes 1769476

commit v2 on v1

v2 whole, which is shorter than its diff:
```python
import jax
import jax.numpy as jnp
from jax import lax
from jax.experimental import pallas as pl
from jax.experimental.pallas import tpu as pltpu
from jax.sharding import PartitionSpec as P

MESH = pl.DeviceIdType.MESH
F32 = jnp.float32
BF16 = jnp.bfloat16
NODES = 3
SN = 512
HALF = 256
PIECE = 96
ROWS = 1536
COLS = 768
QUARTER = 128


def pair_index(later, earlier):
    return later * (later - 1) // 2 + earlier


def split(value):
    high = value.astype(BF16)
    return high, (value - high.astype(F32)).astype(BF16)


def dot(left, right):
    return jnp.dot(left, right, preferred_element_type=F32)


def dot3(left, right_high, right_low):
    high, low = split(left)
    return dot(high, right_high) + dot(high, right_low) + dot(low, right_high)


def first_block(node):
    return node * (node + 1) // 2


def kernel(
    inverse, factor, coupling, diagonal, ancestors,
    rows_out, columns_out, blocks_out,
    inv, inv_high, inv_low, own_masked, lower, partial, traded, arrived, solved,
    couple, couple_high, couple_low, diag, tail, side, side_high, side_low,
    column_lower, tilde_high, tilde_low, inner, inner_recv, inner_sum, inner_last,
    local_sem, gather_send, gather_recv, lower_sem, spread_send, spread_recv, both_sem, columns_sem, trade_sem,
    sum_send, sum_recv, rows_send, rows_recv, swap_sem, down_send, down_recv, up_send, up_recv, pair_send, pair_recv,
):
    row = lax.axis_index("row")
    col = lax.axis_index("col")
    y, core, z, x = row // 2, row % 2, col // 4, col % 4

    def device(dy=0, dcore=0, dz=0, dx=0):
        return (
            ((y + dy) % 4) * 2 + (core + dcore) % 2,
            ((z + dz) % 4) * 4 + (x + dx) % 4,
        )

    def along(axis, step):
        return device(**{"d" + axis: step % 4})

    coordinate = {"x": x, "y": y, "z": z}
    partner = device(dcore=1)
    forward = (col // 2, (col % 2) * 8 + row)
    backward = (col % 8, 2 * row + col // 8)
    moves = jnp.logical_or(forward[0] != row, forward[1] != col)
    lower_to = (x * 2 + z % 2, y * 4 + 2 * core + z // 2)
    lower_from = (z * 2 + x // 2, (2 * (x % 2) + core) * 4 + y)
    lower_moves = jnp.logical_or(lower_to[0] != row, lower_to[1] != col)

    sent = []
    copies = {}

    def remote(src, dst, send_sem, recv_sem, target):
        return pltpu.make_async_remote_copy(
            src_ref=src, dst_ref=dst, send_sem=send_sem, recv_sem=recv_sem,
            device_id=target, device_id_type=MESH,
        )

    def start(src, dst, send_sem, recv_sem, target):
        copy = remote(src, dst, send_sem, recv_sem, target)
        copy.start()
        sent.append(copy)
        return copy

    barrier = pltpu.get_barrier_semaphore()
    neighbours = [along(a, s) for a in "xyz" for s in (1, 2, 3)] + [partner]
    for target in neighbours:
        pl.semaphore_signal(barrier, inc=1, device_id=target, device_id_type=MESH)

    @pl.when(moves)
    def _():
        for target in (forward, backward):
            pl.semaphore_signal(barrier, inc=1, device_id=target, device_id_type=MESH)

    @pl.when(lower_moves)
    def _():
        for target in (lower_to, lower_from):
            pl.semaphore_signal(barrier, inc=1, device_id=target, device_id_type=MESH)

    load_inv = pltpu.make_async_copy(inverse, inv, local_sem.at[0])
    load_couple = pltpu.make_async_copy(coupling, couple, local_sem.at[1])
    load_diag = pltpu.make_async_copy(diagonal, diag, local_sem.at[2])
    load_inv.start()
    load_couple.start()
    load_diag.start()

    first_row = (row * 16 + col) * PIECE
    block_first = first_row // SN
    block_last = (first_row + PIECE - 1) // SN
    row_at = first_row + lax.broadcasted_iota(jnp.int32, (PIECE, SN), 0)
    in_first = row_at < (block_first + 1) * SN
    for node in range(NODES):
        first_listed = jnp.float32(0)
        last_listed = jnp.float32(0)
        for slot in range(24):
            entry = ancestors[node, slot]
            first_listed = jnp.where(entry == block_first, 1.0, first_listed)
            last_listed = jnp.where(entry == block_last, 1.0, last_listed)
        keep = jnp.where(in_first, first_listed, last_listed)
        masked = jnp.where(keep > 0.5, factor[node].astype(F32), 0.0).astype(BF16)
        own_masked[node] = masked
        lower[node, 0, z, x] = masked[:, :HALF]
        lower[node, 1, z, x] = masked[:, HALF:]

    pl.semaphore_wait(
        barrier, len(neighbours) + 2 * jnp.where(moves, 1, 0) + 2 * jnp.where(lower_moves, 1, 0)
    )

    def piece(node, half, first, second):
        return lower.at[node, half, second, first] if half == 0 else lower.at[node, half, first, second]

    def line(node, half, second):
        return lower.at[node, half, second] if half == 0 else lower.at[node, half, :, second]

    def line_part(node, half, second, part):
        where = pl.ds(2 * part, 2)
        return lower.at[node, half, second, where] if half == 0 else lower.at[node, half, where, second]

    axes = ("xz", "zx")

    def gather_copy(node, half, index, ref, axis, step):
        return start(
            ref, ref, gather_send.at[node, half, index], gather_recv.at[node, half, index], along(axis, step)
        )

    def first_phase(node):
        for half in range(2):
            a = axes[half][0]
            own = piece(node, half, coordinate[a], coordinate[axes[half][1]])
            copies[node, half, 0] = gather_copy(node, half, 0, own, a, 1)
            copies[node, half, 1] = gather_copy(node, half, 1, own, a, 3)

    def first_forward(node):
        for half in range(2):
            a, b = axes[half]
            for index, shift, step, cut in ((0, 3, 1, 0), (1, 1, 3, 128)):
                copies[node, half, index].wait_recv()
                got = piece(node, half, (coordinate[a] + shift) % 4, coordinate[b])
                copies[node, half, index + 2] = gather_copy(
                    node, half, index + 2, got.at[:, pl.ds(cut, 128)], a, step
                )

    def second_phase(node):
        for half in range(2):
            b = axes[half][1]
            copies[node, half, 2].wait_recv()
            copies[node, half, 3].wait_recv()
            own = line(node, half, coordinate[b])
            copies[node, half, 4] = gather_copy(node, half, 4, own, b, 1)
            copies[node, half, 5] = gather_copy(node, half, 5, own, b, 3)

    def second_forward(node):
        for half in range(2):
            b = axes[half][1]
            for index, shift, step, part in ((4, 3, 1, 0), (5, 1, 3, 1)):
                copies[node, half, index].wait_recv()
                got = line_part(node, half, (coordinate[b] + shift) % 4, part)
                copies[node, half, index + 2] = gather_copy(node, half, index + 2, got, b, step)

    def gathered(node, half):
        copies[node, half, 6].wait_recv()
        copies[node, half, 7].wait_recv()

    def multiply(node):
        for half in range(2):
            gathered(node, half)
            right = lower[node, half].reshape(ROWS, HALF)
            for part in range(4):
                rows = pl.ds(part * 192, 192)
                product = dot(inv_high[rows, :], right) + dot(inv_low[rows, :], right)
                partial[node, part, :, :, half * HALF : (half + 1) * HALF] = product.reshape(2, PIECE, HALF)
        copies["trade", node] = start(
            partial.at[node, :, 1 - core], traded.at[node], trade_sem.at[node, 0], trade_sem.at[node, 1], partner
        )

    def chain(later, earlier):
        g = pair_index(later, earlier)

        def body(part, carry):
            partial[later, part, core] = partial[later, part, core] + dot3(
                traded[earlier, part], couple_high[g], couple_low[g]
            )
            return carry

        lax.fori_loop(0, 4, body, 0)

    def reduce_start(node):
        copies["trade", node].wait_recv()
        traded[node] = -(traded[node] + partial[node, :, core])
        for step in (1, 2, 3):
            at = pl.multiple_of((y + step) % 4 * QUARTER, QUARTER)
            copies["sum", node, step] = start(
                traded.at[node, :, :, pl.ds(at, QUARTER)], arrived.at[node, step - 1],
                sum_send.at[node, step - 1], sum_recv.at[node, step - 1], along("y", step),
            )

    def finish(node):
        at = pl.multiple_of(y * QUARTER, QUARTER)
        total = traded[node, :, :, pl.ds(at, QUARTER)]
        for step in (1, 2, 3):
            copies["sum", node, step].wait_recv()
            total = total + arrived[node, step - 1]
        solved[node, :, core] = total
        ref = solved.at[node, :, core]
        copies["swap", node] = start(ref, ref, swap_sem.at[node, 0], swap_sem.at[node, 1], partner)

    def rows_start(node):
        at = pl.multiple_of(y * QUARTER, QUARTER)
        where = (node, slice(None), pl.ds(at, QUARTER))
        for step in (1, 2, 3):
            copies["rows", node, step] = start(
                solved.at[node, (y + step) % 4, core], rows_out.at[where],
                rows_send.at[node, step - 1], rows_recv.at[node, step - 1], along("y", step),
            )
        rows_out[where] = solved[node, y, core]

    def columns_copy(node):
        return remote(
            rows_out.at[node], columns_out.at[node], columns_sem.at[node, 0], columns_sem.at[node, 1], forward
        )

    def columns_start(node):
        for step in (1, 2, 3):
            copies["rows", node, step].wait_recv()

        @pl.when(moves)
        def _():
            columns_copy(node).start()

        @pl.when(jnp.logical_not(moves))
        def _():
            columns_out[node] = rows_out[node]

    def columns_wait(node):
        @pl.when(moves)
        def _():
            columns_copy(node).wait()

    def lower_copy():
        return remote(
            own_masked, column_lower.at[:, z % 2, x], lower_sem.at[0], lower_sem.at[1], lower_to
        )

    def lower_start():
        @pl.when(lower_moves)
        def _():
            lower_copy().start()

        @pl.when(jnp.logical_not(lower_moves))
        def _():
            for node in range(NODES):
                column_lower[node, core, y] = own_masked[node]

    def lower_spread():
        @pl.when(lower_moves)
        def _():
            lower_copy().wait()

        ref = column_lower.at[:, core, y]
        for step in (1, 2, 3):
            copies["spread", step] = start(
                ref, ref, spread_send.at[step - 1], spread_recv.at[step - 1], along("y", step)
            )

    def lower_both():
        for step in (1, 2, 3):
            copies["spread", step].wait_recv()
        ref = column_lower.at[:, core]
        copies["both"] = start(ref, ref, both_sem.at[0], both_sem.at[1], partner)

    def prepare_tilde():
        copies["both"].wait_recv()
        for side_core in range(2):
            for part in range(4):
                rows = pl.ds((side_core * 4 + part) * PIECE, PIECE)
                for node in range(NODES):
                    own = column_lower[node, side_core, part]
                    if node == 0:
                        tilde_high[0, rows, :] = own
                        continue
                    first = column_lower[0, side_core, part]
                    g = pair_index(node, 0)
                    value = own.astype(F32) - (dot(first, couple_high[g]) + dot(first, couple_low[g]))
                    if node == 2:
                        high, low = tilde_high[1, rows, :], tilde_low[1, rows, :]
                        g = pair_index(2, 1)
                        value = value - (
                            dot(high, couple_high[g]) + dot(high, couple_low[g]) + dot(low, couple_high[g])
                        )
                    high, low = split(value)
                    tilde_high[node, rows, :] = high
                    tilde_low[node, rows, :] = low

    def inner_products(later):
        copies["swap", later].wait_recv()
        high, low = split(solved[later].reshape(COLS, QUARTER).T)
        mine = pl.ds(pl.multiple_of(core * HALF, HALF), HALF)
        for earlier in range(later + 1):
            right = tilde_high[earlier, :, mine]
            value = dot(high, right) + dot(low, right)
            if earlier > 0:
                value = value + dot(high, tilde_low[earlier, :, mine])
            for half in range(2):
                cut = value[:, half * QUARTER : (half + 1) * QUARTER]
                inner[half, first_block(later) + earlier] = -cut.reshape(4, 4, 8, QUARTER)

    def down_start(node, level):
        group = slice(first_block(node), first_block(node) + node + 1)
        for half in range(2):
            axis = ("xz", "zx")[half][level]
            for step in (1, 2, 3):
                target = (coordinate[axis] + step) % 4
                if level == 1:
                    src, dst = inner_sum.at[half, group, target], inner_last.at[half, step - 1, group]
                else:
                    src = inner.at[0, group, target] if half == 0 else inner.at[1, group, :, target]
                    dst = inner_recv.at[half, step - 1, group]
                sems = (node, level, half, step - 1)
                copies["down", node, level, half, step] = start(
                    src, dst, down_send.at[sems], down_recv.at[sems], along(axis, step)
                )

    def down_finish(node, level, half):
        group = slice(first_block(node), first_block(node) + node + 1)
        axis = ("xz", "zx")[half][level]
        own = coordinate[axis]
        if level == 1:
            total = inner_sum[half, group, own]
        else:
            total = inner[0, group, own] if half == 0 else inner[1, group, :, own]
        land = (inner_recv, inner_last)[level]
        for step in (1, 2, 3):
            copies["down", node, level, half, step].wait_recv()
            total = total + land[half, step - 1, group]
        return total

    def down_middle(node):
        group = slice(first_block(node), first_block(node) + node + 1)
        for half in range(2):
            inner_sum[half, group] = down_finish(node, 0, half)
        down_start(node, 1)

    def down_last(node):
        rows = pl.ds(pl.multiple_of(y * 128 + x * 32 + z * 8, 8), 8)
        for half in range(2):
            total = down_finish(node, 1, half)
            lanes = pl.ds(pl.multiple_of(core * HALF + half * QUARTER, QUARTER), QUARTER)
            for earlier in range(node + 1):
                block = first_block(node) + earlier
                blocks_out[block, core, half, y, x, z] = tail[block, rows, lanes] + total[earlier]

    orders = ("zxy", "yzx", "xyz")

    def up_ref(block, level, **other):
        done = orders[block % 3][:level]
        where = [other.get(a, slice(None) if a in done else coordinate[a]) for a in "yxz"]
        return blocks_out.at[(block, core, slice(None), *where)]

    def up_start(block, level):
        axis = orders[block % 3][level]
        ref = up_ref(block, level)
        for step in (1, 2, 3):
            sems = (block, level, step - 1)
            copies["up", block, level, step] = start(ref, ref, up_send.at[sems], up_recv.at[sems], along(axis, step))

    def up_wait(block, level):
        for step in (1, 2, 3):
            copies["up", block, level, step].wait_recv()

    def pair_start(block, step):
        axis = orders[block % 3][2]
        ref = up_ref(block, 2, **{axis: (coordinate[axis] - step) % 4})
        copies["pair", block, step] = start(ref, ref, pair_send.at[block, step], pair_recv.at[block, step], partner)

    def up_all(group):
        for level in range(3):
            for block in group:
                if level > 0:
                    up_wait(block, level - 1)
                up_start(block, level)
                if level == 2:
                    pair_start(block, 0)

    def pair_rest(group):
        for step in (1, 3, 2):
            for block in group:
                copies["up", block, 2, step].wait_recv()
                pair_start(block, step)

    def split_side(value):
        high, low = split(value)
        side_high[...] = high
        side_low[...] = low

    def add_product(target, left, high, low, base):
        def body(block, carry):
            rows = pl.ds(pl.multiple_of(block * 128, 128), 128)
            target[rows, :] = base[rows, :] - dot3(left[rows, :], high[...], low[...])
            return carry

        lax.fori_loop(0, 4, body, 0)

    def negate_product(target, left, high, low):
        def body(block, carry):
            rows = pl.ds(pl.multiple_of(block * 128, 128), 128)
            target[rows, :] = -dot3(left[rows, :], high[...], low[...])
            return carry

        lax.fori_loop(0, 4, body, 0)

    e00, e01, e11, e02, e12, e22 = (tail.at[i] for i in (0, 1, 2, 3, 4, 5))

    def tail_first():
        e00[...] = diag[0]
        negate_product(e01, diag.at[0], couple_high.at[0], couple_low.at[0])
        negate_product(e02, diag.at[0], couple_high.at[1], couple_low.at[1])
        add_product(e02, e01, couple_high.at[2], couple_low.at[2], e02)

    def tail_second():
        split_side(e01[...])
        side[...] = couple[0].T
        add_product(e11, side, side_high, side_low, diag.at[1])
        e01[...] = e01[...].T
        negate_product(e12, e01, couple_high.at[1], couple_low.at[1])
        add_product(e12, e11, couple_high.at[2], couple_low.at[2], e12)

    def tail_third():
        split_side(e02[...])
        side[...] = couple[1].T
        add_product(e22, side, side_high, side_low, diag.at[2])
        split_side(e12[...])
        side[...] = couple[2].T
        add_product(e22, side, side_high, side_low, e22)
        e02[...] = e02[...].T
        e12[...] = e12[...].T

    for node in range(NODES):
        first_phase(node)
    load_inv.wait()
    first_forward(0)
    second_phase(0)
    first_forward(1)
    first_forward(2)
    lower_start()
    for block in range(6):
        where = slice(block * 256, (block + 1) * 256)
        high, low = split(inv[where, :].T)
        inv_high[:, where] = high
        inv_low[:, where] = low
    second_forward(0)
    second_phase(1)
    load_couple.wait()
    load_diag.wait()
    for g in range(3):
        high, low = split(couple[g])
        couple_high[g] = high
        couple_low[g] = low
    multiply(0)
    second_forward(1)
    second_phase(2)
    lower_spread()
    reduce_start(0)
    tail_first()
    multiply(1)
    chain(1, 0)
    second_forward(2)
    lower_both()
    reduce_start(1)
    finish(0)
    rows_start(0)
    tail_second()
    multiply(2)
    chain(2, 0)
    chain(2, 1)
    reduce_start(2)
    columns_start(0)
    prepare_tilde()
    inner_products(0)
    down_start(0, 0)
    finish(1)
    rows_start(1)
    inner_products(1)
    down_start(1, 0)
    tail_third()
    down_middle(0)
    down_middle(1)
    columns_start(1)
    down_last(0)
    down_last(1)
    up_all((0, 1, 2))
    finish(2)
    rows_start(2)
    inner_products(2)
    down_start(2, 0)
    pair_rest((0, 1, 2))
    down_middle(2)
    columns_start(2)
    down_last(2)
    up_all((3, 4, 5))
    pair_rest((3, 4, 5))
    for block in range(6):
        for step in range(4):
            copies["pair", block, step].wait_recv()
    for node in range(NODES):
        columns_wait(node)
    for copy in sent:
        copy.wait_send()


def fused(ancestor_inverse, factor, coupling, diagonal_inverse, ancestors):
    vmem = pl.BlockSpec(memory_space=pltpu.VMEM)
    hbm = pl.BlockSpec(memory_space=pl.ANY)
    dma = pltpu.SemaphoreType.DMA
    square = (SN, SN)
    return pl.pallas_call(
        kernel,
        out_shape=(
            jax.ShapeDtypeStruct((NODES, PIECE, SN), F32),
            jax.ShapeDtypeStruct((NODES, PIECE, SN), F32),
            jax.ShapeDtypeStruct((6, 2, 2, 4, 4, 4, 8, QUARTER), F32),
        ),
        in_specs=[hbm, vmem, hbm, hbm, pl.BlockSpec(memory_space=pltpu.SMEM)],
        out_specs=(vmem, vmem, vmem),
        scratch_shapes=[
            pltpu.VMEM((ROWS, COLS), F32),
            pltpu.VMEM((COLS, ROWS), BF16),
            pltpu.VMEM((COLS, ROWS), BF16),
            pltpu.VMEM((NODES, PIECE, SN), BF16),
            pltpu.VMEM((NODES, 2, 4, 4, PIECE, HALF), BF16),
            pltpu.VMEM((NODES, 4, 2, PIECE, SN), F32),
            pltpu.VMEM((NODES, 4, PIECE, SN), F32),
            pltpu.VMEM((NODES, 3, 4, PIECE, QUARTER), F32),
            pltpu.VMEM((NODES, 4, 2, PIECE, QUARTER), F32),
            pltpu.VMEM((3,) + square, F32),
            pltpu.VMEM((3,) + square, BF16),
            pltpu.VMEM((3,) + square, BF16),
            pltpu.VMEM((3,) + square, F32),
            pltpu.VMEM((6,) + square, F32),
            pltpu.VMEM(square, F32),
            pltpu.VMEM(square, BF16),
            pltpu.VMEM(square, BF16),
            pltpu.VMEM((NODES, 2, 4, PIECE, SN), BF16),
            pltpu.VMEM((NODES, COLS, SN), BF16),
            pltpu.VMEM((NODES, COLS, SN), BF16),
            pltpu.VMEM((2, 6, 4, 4, 8, QUARTER), F32),
            pltpu.VMEM((2, 3, 6, 4, 8, QUARTER), F32),
            pltpu.VMEM((2, 6, 4, 8, QUARTER), F32),
            pltpu.VMEM((2, 3, 6, 8, QUARTER), F32),
            dma((3,)),
            dma((NODES, 2, 8)),
            dma((NODES, 2, 8)),
            dma((2,)),
            dma((3,)),
            dma((3,)),
            dma((2,)),
            dma((NODES, 2)),
            dma((NODES, 2)),
            dma((NODES, 3)),
            dma((NODES, 3)),
            dma((NODES, 3)),
            dma((NODES, 3)),
            dma((NODES, 2)),
            dma((NODES, 2, 2, 3)),
            dma((NODES, 2, 2, 3)),
            dma((6, 3, 3)),
            dma((6, 3, 3)),
            dma((6, 4)),
            dma((6, 4)),
        ],
        compiler_params=pltpu.CompilerParams(
            collective_id=0, has_side_effects=True, vmem_limit_bytes=63 << 20
        ),
        name="selected_inversion",
    )(ancestor_inverse, factor, coupling, diagonal_inverse, ancestors)


def assemble_kernel(block, out):
    def lanes(half):
        return block[0, half // 2, half % 2].reshape(SN, QUARTER)

    upper = pl.program_id(0) < pl.program_id(1)

    @pl.when(jnp.logical_not(upper))
    def _():
        for half in range(4):
            out[0, 0, :, half * QUARTER : (half + 1) * QUARTER] = lanes(half)

    @pl.when(upper)
    def _():
        for half in range(4):
            out[0, 0, half * QUARTER : (half + 1) * QUARTER, :] = lanes(half).T


def assemble(blocks):
    def at(first, second):
        later, earlier = jnp.maximum(first, second), jnp.minimum(first, second)
        return (later * (later + 1) // 2 + earlier,) + (0,) * 7

    return pl.pallas_call(
        assemble_kernel,
        out_shape=jax.ShapeDtypeStruct((NODES, NODES, SN, SN), F32),
        grid=(NODES, NODES),
        in_specs=[pl.BlockSpec((1, 2, 2, 4, 4, 4, 8, QUARTER), at)],
        out_specs=pl.BlockSpec((1, 1, SN, SN), lambda first, second: (first, second, 0, 0)),
        compiler_params=pltpu.CompilerParams(vmem_limit_bytes=16 << 20),
        name="assemble_node_blocks",
    )(blocks)


def local(ancestor_inverse, factor, coupling, diagonal_inverse, ancestors):
    block_rows, block_columns, blocks = fused(
        ancestor_inverse, factor, coupling, diagonal_inverse, ancestors
    )
    return block_columns, block_rows, assemble(blocks)


def solution(mesh):
    placed = (P("row", "col"), P(None, ("row", "col"), None), P(), P(), P())
    return jax.shard_map(
        local,
        mesh=mesh,
        in_specs=placed,
        out_specs=(P(None, ("row", "col"), None), P(None, ("col", "row"), None), P()),
        check_vma=False,
    )
```

time: 178 us -> 168 us (0.944)
  other arithmetic: 8.19 us -> 0 us
  Pallas kernels: 156 us -> 163 us
  local copies, waits for them, and re-layouts: 11.2 us -> 4.41 us
    another operation x3 -> x0, other arithmetic: 8.19 us -> none  [local(): jnp.stack([jnp.stack([blocks[j, k] for k in range(NODES)]) for j in range...]
    pallas_call x0 -> x1, Pallas kernels: none -> 5.75 us  [assemble(): pl.pallas_call(assemble_kernel, out_shape=jax.ShapeDtypeStruct((NODES, NO...]
    slice x1 -> x0, local copies, waits for them, and re-layouts: 5.09 us -> none  [local(): part = upper[:, index // 2, index % 2 * HALF:(index % 2 + 1) * HALF]]
    another operation x3 -> x0, local copies, waits for them, and re-layouts: 3.99 us -> none  [local(): blocks[earlier, later] = part.reshape(SN, SN)]
    unnamed x12 -> x8, local copies, waits for them, and re-layouts: 2.1 us -> 4.41 us
where the time goes in v2:
time: 168 us
  Pallas kernels  163 us (97%)
  local copies, waits for them, and re-layouts  4.41 us (3%)
    pallas_call x1, Pallas kernels, fused(): pl.pallas_call(kernel, out_shape=(jax.ShapeDtypeStruct((NODES, PIECE, SN)...  157 us
    pallas_call x1, Pallas kernels, assemble(): pl.pallas_call(assemble_kernel, out_shape=jax.ShapeDtypeStruct((NODES, NO...  5.75 us
    unnamed x8, local copies, waits for them, and re-layouts  4.41 us

profile of v2, /device:TPU:1, one launch (start us, length us, event | category | flops | bytes accessed | tf_op | source)
XLA Modules:
  0.0 167.6 jit_solution(9018727198898164519)
XLA Ops:
  0.6 156.8 %selected_inversion.1 = (f32[3,96,512]{2,1,0:T(8,128)}, f32[3,96,512]{2,1,0:T(8,128)}, f32[6,2,2,4,4,4,8,128]{7,6,5,4,3,2,1,0:T(8,128)}) custom-call(f32[1536,768]{1,0:T(8,128)} %inverse.1, bf16[3,96,512]{2,1,0:T(8,128)(2,1)} %factor.1, f32[3,512,512]{2,1,0:T(8,128)} %coupling.1, f32[3,512,512]{2,1,0:T(8,128)} %diagonal.1, s32[3,24]{1,0:T(4,128)} %ancestors.1), custom_call_target="tpu_custom_call" | custom-call | tf_op jit(solution)/shard_map/selected_inversion/pallas_call | solution.py:538
  157.5 0.0 copy-start
  157.5 2.8 %copy-done = f32[6,2,2,4,4,4,8,128]{7,6,5,4,3,2,1,0:T(8,128)S(1)} copy-done((f32[6,2,2,4,4,4,8,128]{7,6,5,4,3,2,1,0:T(8,128)S(1)}, f32[6,2,2,4,4,4,8,128]{7,6,5,4,3,2,1,0:T(8,128)}, u32[]{:S(2)}) %copy-start) | copy-done | bytes 6291480
  160.2 0.0 copy-start.2
  160.2 0.0 copy-start.1
  160.2 5.7 %assemble_node_blocks.1 = f32[3,3,512,512]{3,2,1,0:T(8,128)} custom-call(f32[6,2,2,4,4,4,8,128]{7,6,5,4,3,2,1,0:T(8,128)S(1)} %copy-done), custom_call_target="tpu_custom_call" | custom-call | tf_op jit(solution)/shard_map/assemble_node_blocks/pallas_call | solution.py:622
  166.0 0.0 copy-done.2
  166.0 0.8 copy.10
  166.8 0.0 copy-done.1
  166.8 0.8 copy.11
Async XLA Ops:
  157.5 2.8 %copy-start = (f32[6,2,2,4,4,4,8,128]{7,6,5,4,3,2,1,0:T(8,128)S(1)}, f32[6,2,2,4,4,4,8,128]{7,6,5,4,3,2,1,0:T(8,128)}, u32[]{:S(2)}) copy-start(f32[6,2,2,4,4,4,8,128]{7,6,5,4,3,2,1,0:T(8,128)} %get-tuple-element.8.block) | copy-start | bytes 18874372
  160.2 5.8 %copy-start.2 = (f32[3,96,512]{2,1,0:T(8,128)S(1)}, f32[3,96,512]{2,1,0:T(8,128)}, u32[]{:S(2)}) copy-start(f32[3,96,512]{2,1,0:T(8,128)} %get-tuple-element.12) | copy-start | bytes 1769476
  160.2 6.6 %copy-start.1 = (f32[3,96,512]{2,1,0:T(8,128)S(1)}, f32[3,96,512]{2,1,0:T(8,128)}, u32[]{:S(2)}) copy-start(f32[3,96,512]{2,1,0:T(8,128)} %get-tuple-element.13) | copy-start | bytes 1769476

commit v3 on v2

--- a/solution.py
+++ b/solution.py
@@ -42,7 +42,7 @@
 def kernel(
     inverse, factor, coupling, diagonal, ancestors,
     rows_out, columns_out, blocks_out,
-    inv, inv_high, inv_low, own_masked, lower, partial, traded, arrived, solved,
+    inv, inv_high, inv_low, own_masked, lower, partial, traded, correct, arrived, solved,
     couple, couple_high, couple_low, diag, tail, side, side_high, side_low,
     column_lower, tilde_high, tilde_low, inner, inner_recv, inner_sum, inner_last,
     local_sem, gather_send, gather_recv, lower_sem, spread_send, spread_recv, both_sem, columns_sem, trade_sem,
@@ -200,16 +200,18 @@
         g = pair_index(later, earlier)
 
         def body(part, carry):
-            partial[later, part, core] = partial[later, part, core] + dot3(
-                traded[earlier, part], couple_high[g], couple_low[g]
-            )
+            value = dot3(traded[earlier, part], couple_high[g], couple_low[g])
+            correct[later, part] = value if earlier == 0 else correct[later, part] + value
             return carry
 
         lax.fori_loop(0, 4, body, 0)
 
     def reduce_start(node):
         copies["trade", node].wait_recv()
-        traded[node] = -(traded[node] + partial[node, :, core])
+        total = traded[node] + partial[node, :, core]
+        if node > 0:
+            total = total + correct[node]
+        traded[node] = -total
         for step in (1, 2, 3):
             at = pl.multiple_of((y + step) % 4 * QUARTER, QUARTER)
             copies["sum", node, step] = start(
@@ -364,13 +366,12 @@
         down_start(node, 1)
 
     def down_last(node):
-        rows = pl.ds(pl.multiple_of(y * 128 + x * 32 + z * 8, 8), 8)
         for half in range(2):
             total = down_finish(node, 1, half)
             lanes = pl.ds(pl.multiple_of(core * HALF + half * QUARTER, QUARTER), QUARTER)
             for earlier in range(node + 1):
                 block = first_block(node) + earlier
-                blocks_out[block, core, half, y, x, z] = tail[block, rows, lanes] + total[earlier]
+                blocks_out[block, core, half, y, x, z] = tail[block, :, lanes] + total[earlier]
 
     orders = ("zxy", "yzx", "xyz")
 
@@ -394,15 +395,6 @@
         axis = orders[block % 3][2]
         ref = up_ref(block, 2, **{axis: (coordinate[axis] - step) % 4})
         copies["pair", block, step] = start(ref, ref, pair_send.at[block, step], pair_recv.at[block, step], partner)
-
-    def up_all(group):
-        for level in range(3):
-            for block in group:
-                if level > 0:
-                    up_wait(block, level - 1)
-                up_start(block, level)
-                if level == 2:
-                    pair_start(block, 0)
 
     def pair_rest(group):
         for step in (1, 3, 2):
@@ -410,61 +402,56 @@
                 copies["up", block, 2, step].wait_recv()
                 pair_start(block, step)
 
-    def split_side(value):
-        high, low = split(value)
+    finished = pl.ds(pl.multiple_of(y * 128 + x * 32 + z * 8, 8), 8)
+
+    def dot3_t(left, right_high, right_low):
+        def across(a, b):
+            return lax.dot_general(a, b, (((1,), (1,)), ((), ())), preferred_element_type=F32)
+
+        high, low = split(left)
+        return across(high, right_high) + across(high, right_low) + across(low, right_high)
+
+    def split_diag(index):
+        high, low = split(diag[index])
         side_high[...] = high
         side_low[...] = low
 
-    def add_product(target, left, high, low, base):
-        def body(block, carry):
-            rows = pl.ds(pl.multiple_of(block * 128, 128), 128)
-            target[rows, :] = base[rows, :] - dot3(left[rows, :], high[...], low[...])
-            return carry
-
-        lax.fori_loop(0, 4, body, 0)
-
-    def negate_product(target, left, high, low):
-        def body(block, carry):
-            rows = pl.ds(pl.multiple_of(block * 128, 128), 128)
-            target[rows, :] = -dot3(left[rows, :], high[...], low[...])
-            return carry
-
-        lax.fori_loop(0, 4, body, 0)
-
-    e00, e01, e11, e02, e12, e22 = (tail.at[i] for i in (0, 1, 2, 3, 4, 5))
-
-    def tail_first():
-        e00[...] = diag[0]
-        negate_product(e01, diag.at[0], couple_high.at[0], couple_low.at[0])
-        negate_product(e02, diag.at[0], couple_high.at[1], couple_low.at[1])
-        add_product(e02, e01, couple_high.at[2], couple_low.at[2], e02)
-
-    def tail_second():
-        split_side(e01[...])
-        side[...] = couple[0].T
-        add_product(e11, side, side_high, side_low, diag.at[1])
-        e01[...] = e01[...].T
-        negate_product(e12, e01, couple_high.at[1], couple_low.at[1])
-        add_product(e12, e11, couple_high.at[2], couple_low.at[2], e12)
-
-    def tail_third():
-        split_side(e02[...])
-        side[...] = couple[1].T
-        add_product(e22, side, side_high, side_low, diag.at[2])
-        split_side(e12[...])
-        side[...] = couple[2].T
-        add_product(e22, side, side_high, side_low, e22)
-        e02[...] = e02[...].T
-        e12[...] = e12[...].T
+    def tail_terms():
+        taken = []
+        for g in range(3):
+            side[...] = couple[g].T
+            taken.append(side[finished, :])
+        first, second, third = taken
+        ch, cl = couple_high, couple_low
+        mixed = dot3_t(third, ch[0], cl[0])
+        stacked = jnp.concatenate([first, second, mixed], axis=0)
+        split_diag(0)
+        plain = dot3(stacked, side_high[...], side_low[...])
+        turned = dot3_t(stacked, side_high[...], side_low[...])
+        split_diag(1)
+        after = dot3(third, side_high[...], side_low[...])
+        after_t = dot3_t(third, side_high[...], side_low[...])
+        a1, a2, a3 = plain[0:8], plain[8:16], plain[16:24]
+        b1, b2, b3 = turned[0:8], turned[8:16], turned[16:24]
+        through = dot3(jnp.concatenate([a1, a2, b3, a3], axis=0), ch[0], cl[0])
+        e1, e2, e3, e4 = through[0:8], through[8:16], through[16:24], through[24:32]
+        tail[0] = diag[0, finished, :]
+        tail[1] = -b1
+        tail[2] = diag[1, finished, :] + e1
+        tail[3] = b3 - b2
+        tail[4] = e2 - after_t - e3
+        tail[5] = (
+            diag[2, finished, :] + dot3(a2 - b3, ch[1], cl[1]) + dot3(after + e4 - e2, ch[2], cl[2])
+        )
 
     for node in range(NODES):
         first_phase(node)
-    load_inv.wait()
+    lower_start()
     first_forward(0)
     second_phase(0)
     first_forward(1)
     first_forward(2)
-    lower_start()
+    load_inv.wait()
     for block in range(6):
         where = slice(block * 256, (block + 1) * 256)
         high, low = split(inv[where, :].T)
@@ -472,6 +459,7 @@
         inv_low[:, where] = low
     second_forward(0)
     second_phase(1)
+    lower_spread()
     load_couple.wait()
     load_diag.wait()
     for g in range(3):
@@ -481,45 +469,58 @@
     multiply(0)
     second_forward(1)
     second_phase(2)
-    lower_spread()
     reduce_start(0)
-    tail_first()
+    chain(1, 0)
     multiply(1)
-    chain(1, 0)
     second_forward(2)
     lower_both()
     reduce_start(1)
+    chain(2, 0)
+    chain(2, 1)
     finish(0)
     rows_start(0)
-    tail_second()
     multiply(2)
-    chain(2, 0)
-    chain(2, 1)
+    prepare_tilde()
     reduce_start(2)
-    columns_start(0)
-    prepare_tilde()
     inner_products(0)
     down_start(0, 0)
     finish(1)
     rows_start(1)
     inner_products(1)
     down_start(1, 0)
-    tail_third()
+    columns_start(0)
+    tail_terms()
     down_middle(0)
     down_middle(1)
     columns_start(1)
     down_last(0)
     down_last(1)
-    up_all((0, 1, 2))
+    for block in (0, 1, 2):
+        up_start(block, 0)
     finish(2)
     rows_start(2)
     inner_products(2)
     down_start(2, 0)
-    pair_rest((0, 1, 2))
+    for block in (0, 1, 2):
+        up_wait(block, 0)
+        up_start(block, 1)
     down_middle(2)
     columns_start(2)
+    for block in (0, 1, 2):
+        up_wait(block, 1)
+        up_start(block, 2)
+        pair_start(block, 0)
     down_last(2)
-    up_all((3, 4, 5))
+    for block in (3, 4, 5):
+        up_start(block, 0)
+    for block in (3, 4, 5):
+        up_wait(block, 0)
+        up_start(block, 1)
+    for block in (3, 4, 5):
+        up_wait(block, 1)
+        up_start(block, 2)
+        pair_start(block, 0)
+    pair_rest((0, 1, 2))
     pair_rest((3, 4, 5))
     for block in range(6):
         for step in range(4):
@@ -552,13 +553,14 @@
             pltpu.VMEM((NODES, 2, 4, 4, PIECE, HALF), BF16),
             pltpu.VMEM((NODES, 4, 2, PIECE, SN), F32),
             pltpu.VMEM((NODES, 4, PIECE, SN), F32),
+            pltpu.VMEM((NODES, 4, PIECE, SN), F32),
             pltpu.VMEM((NODES, 3, 4, PIECE, QUARTER), F32),
             pltpu.VMEM((NODES, 4, 2, PIECE, QUARTER), F32),
             pltpu.VMEM((3,) + square, F32),
             pltpu.VMEM((3,) + square, BF16),
             pltpu.VMEM((3,) + square, BF16),
             pltpu.VMEM((3,) + square, F32),
-            pltpu.VMEM((6,) + square, F32),
+            pltpu.VMEM((6, 8, SN), F32),
             pltpu.VMEM(square, F32),
             pltpu.VMEM(square, BF16),
             pltpu.VMEM(square, BF16),
@@ -597,44 +599,57 @@
     )(ancestor_inverse, factor, coupling, diagonal_inverse, ancestors)
 
 
-def assemble_kernel(block, out):
+def assemble_kernel(blocks, rows, columns, out, rows_out, columns_out):
+    first, second = pl.program_id(0), pl.program_id(1)
+    later, earlier = jnp.maximum(first, second), jnp.minimum(first, second)
+    block = later * (later + 1) // 2 + earlier
+
     def lanes(half):
-        return block[0, half // 2, half % 2].reshape(SN, QUARTER)
-
-    upper = pl.program_id(0) < pl.program_id(1)
-
-    @pl.when(jnp.logical_not(upper))
+        return blocks[block, half // 2, half % 2].reshape(SN, QUARTER)
+
+    @pl.when(jnp.logical_and(first == 0, second == 0))
+    def _():
+        rows_out[...] = rows[...]
+        columns_out[...] = columns[...]
+
+    @pl.when(first >= second)
     def _():
         for half in range(4):
             out[0, 0, :, half * QUARTER : (half + 1) * QUARTER] = lanes(half)
 
-    @pl.when(upper)
+    @pl.when(first < second)
     def _():
         for half in range(4):
             out[0, 0, half * QUARTER : (half + 1) * QUARTER, :] = lanes(half).T
 
 
-def assemble(blocks):
-    def at(first, second):
-        later, earlier = jnp.maximum(first, second), jnp.minimum(first, second)
-        return (later * (later + 1) // 2 + earlier,) + (0,) * 7
-
+def assemble(blocks, rows, columns):
+    whole = pl.BlockSpec(memory_space=pltpu.VMEM)
     return pl.pallas_call(
         assemble_kernel,
-        out_shape=jax.ShapeDtypeStruct((NODES, NODES, SN, SN), F32),
+        out_shape=(
+            jax.ShapeDtypeStruct((NODES, NODES, SN, SN), F32),
+            jax.ShapeDtypeStruct(rows.shape, F32),
+            jax.ShapeDtypeStruct(columns.shape, F32),
+        ),
         grid=(NODES, NODES),
-        in_specs=[pl.BlockSpec((1, 2, 2, 4, 4, 4, 8, QUARTER), at)],
-        out_specs=pl.BlockSpec((1, 1, SN, SN), lambda first, second: (first, second, 0, 0)),
-        compiler_params=pltpu.CompilerParams(vmem_limit_bytes=16 << 20),
+        in_specs=[whole, whole, whole],
+        out_specs=(
+            pl.BlockSpec((1, 1, SN, SN), lambda first, second: (first, second, 0, 0)),
+            pl.BlockSpec(rows.shape, lambda first, second: (0, 0, 0)),
+            pl.BlockSpec(columns.shape, lambda first, second: (0, 0, 0)),
+        ),
+        compiler_params=pltpu.CompilerParams(vmem_limit_bytes=24 << 20),
         name="assemble_node_blocks",
-    )(blocks)
+    )(blocks, rows, columns)
 
 
 def local(ancestor_inverse, factor, coupling, diagonal_inverse, ancestors):
     block_rows, block_columns, blocks = fused(
         ancestor_inverse, factor, coupling, diagonal_inverse, ancestors
     )
-    return block_columns, block_rows, assemble(blocks)
+    node_blocks, block_rows, block_columns = assemble(blocks, block_rows, block_columns)
+    return block_columns, block_rows, node_blocks
 
 
 def solution(mesh):

time: 168 us -> 150 us (0.89)
  Pallas kernels: 163 us -> 144 us
    pallas_call x1, Pallas kernels: 157 us -> 138 us  [fused(): pl.pallas_call(kernel, out_shape=(jax.ShapeDtypeStruct((NODES, PIECE, SN)...]
    unnamed x8 -> x6, local copies, waits for them, and re-layouts: 4.41 us -> 4.91 us
where the time goes in v3:
time: 150 us; the launch traced here: 149 us
  Pallas kernels  144 us (96%)
  local copies, waits for them, and re-layouts  4.91 us (3%)
    pallas_call x1, Pallas kernels, fused(): pl.pallas_call(kernel, out_shape=(jax.ShapeDtypeStruct((NODES, PIECE, SN)...  138 us
    pallas_call x1, Pallas kernels, assemble(): pl.pallas_call(assemble_kernel, out_shape=(jax.ShapeDtypeStruct((NODES, N...  6.16 us
    unnamed x6, local copies, waits for them, and re-layouts  4.91 us

profile of v3, /device:TPU:1, one launch (start us, length us, event | category | flops | bytes accessed | tf_op | source)
XLA Modules:
  0.0 149.4 jit_solution(4264541380355915565)
XLA Ops:
  0.6 137.7 %selected_inversion.1 = (f32[3,96,512]{2,1,0:T(8,128)}, f32[3,96,512]{2,1,0:T(8,128)}, f32[6,2,2,4,4,4,8,128]{7,6,5,4,3,2,1,0:T(8,128)}) custom-call(f32[1536,768]{1,0:T(8,128)} %inverse.1, bf16[3,96,512]{2,1,0:T(8,128)(2,1)} %factor.1, f32[3,512,512]{2,1,0:T(8,128)} %coupling.1, f32[3,512,512]{2,1,0:T(8,128)} %diagonal.1, s32[3,24]{1,0:T(4,128)} %ancestors.1), custom_call_target="tpu_custom_call" | custom-call | tf_op jit(solution)/shard_map/selected_inversion/pallas_call | solution.py:539
  138.3 0.0 copy-start
  138.3 2.8 %copy-done = f32[6,2,2,4,4,4,8,128]{7,6,5,4,3,2,1,0:T(8,128)S(1)} copy-done((f32[6,2,2,4,4,4,8,128]{7,6,5,4,3,2,1,0:T(8,128)S(1)}, f32[6,2,2,4,4,4,8,128]{7,6,5,4,3,2,1,0:T(8,128)}, u32[]{:S(2)}) %copy-start) | copy-done | bytes 6291480
  141.1 0.0 copy-start.1
  141.1 1.1 copy-done.1
  142.2 0.0 copy-start.2
  142.2 1.1 copy-done.2
  143.2 6.2 %assemble_node_blocks.1 = (f32[3,3,512,512]{3,2,1,0:T(8,128)}, f32[3,96,512]{2,1,0:T(8,128)}, f32[3,96,512]{2,1,0:T(8,128)}) custom-call(f32[6,2,2,4,4,4,8,128]{7,6,5,4,3,2,1,0:T(8,128)S(1)} %copy-done, f32[3,96,512]{2,1,0:T(8,128)S(1)} %copy-done.1, f32[3,96,512]{2,1,0:T(8,128)S(1)} %copy-done.2), custom_call_target="tpu_custom_call" | custom-call | tf_op jit(solution)/shard_map/assemble_node_blocks/pallas_call | solution.py:628
Async XLA Ops:
  138.3 2.8 %copy-start = (f32[6,2,2,4,4,4,8,128]{7,6,5,4,3,2,1,0:T(8,128)S(1)}, f32[6,2,2,4,4,4,8,128]{7,6,5,4,3,2,1,0:T(8,128)}, u32[]{:S(2)}) copy-start(f32[6,2,2,4,4,4,8,128]{7,6,5,4,3,2,1,0:T(8,128)} %get-tuple-element.9.blocks) | copy-start | bytes 18874372
  141.1 1.1 copy-start.1
  142.2 1.1 copy-start.2

commit v4 on v3

--- a/solution.py
+++ b/solution.py
@@ -42,7 +42,7 @@
 def kernel(
     inverse, factor, coupling, diagonal, ancestors,
     rows_out, columns_out, blocks_out,
-    inv, inv_high, inv_low, own_masked, lower, partial, traded, correct, arrived, solved,
+    inv, inv_high, inv_low, own_masked, lower, partial, traded, correct, relay, outgoing, arrived, solved,
     couple, couple_high, couple_low, diag, tail, side, side_high, side_low,
     column_lower, tilde_high, tilde_low, inner, inner_recv, inner_sum, inner_last,
     local_sem, gather_send, gather_recv, lower_sem, spread_send, spread_recv, both_sem, columns_sem, trade_sem,
@@ -212,19 +212,31 @@
         if node > 0:
             total = total + correct[node]
         traded[node] = -total
-        for step in (1, 2, 3):
-            at = pl.multiple_of((y + step) % 4 * QUARTER, QUARTER)
-            copies["sum", node, step] = start(
-                traded.at[node, :, :, pl.ds(at, QUARTER)], arrived.at[node, step - 1],
-                sum_send.at[node, step - 1], sum_recv.at[node, step - 1], along("y", step),
+        for way, step in ((0, 1), (1, 3)):
+            copies["relay", node, way] = start(
+                traded.at[node, pl.ds(2 * way, 2), :, quarter(2)], relay.at[node, way],
+                sum_send.at[node, way], sum_recv.at[node, way], along("y", step),
             )
 
+    def quarter(step):
+        return pl.ds(pl.multiple_of((y + step) % 4 * QUARTER, QUARTER), QUARTER)
+
+    def reduce_relay(node):
+        for way, step in ((0, 1), (1, 3)):
+            copies["relay", node, way].wait_recv()
+            with_relay, plain = (slice(0, 2), slice(2, 4)) if way == 0 else (slice(2, 4), slice(0, 2))
+            outgoing[node, way, with_relay] = traded[node, with_relay, :, quarter(step)] + relay[node, way]
+            outgoing[node, way, plain] = traded[node, plain, :, quarter(step)]
+            copies["sum", node, way] = start(
+                outgoing.at[node, way], arrived.at[node, way],
+                sum_send.at[node, 2 + way], sum_recv.at[node, 2 + way], along("y", step),
+            )
+
     def finish(node):
-        at = pl.multiple_of(y * QUARTER, QUARTER)
-        total = traded[node, :, :, pl.ds(at, QUARTER)]
-        for step in (1, 2, 3):
-            copies["sum", node, step].wait_recv()
-            total = total + arrived[node, step - 1]
+        total = traded[node, :, :, quarter(0)]
+        for way in range(2):
+            copies["sum", node, way].wait_recv()
+            total = total + arrived[node, way]
         solved[node, :, core] = total
         ref = solved.at[node, :, core]
         copies["swap", node] = start(ref, ref, swap_sem.at[node, 0], swap_sem.at[node, 1], partner)
@@ -282,14 +294,20 @@
             lower_copy().wait()
 
         ref = column_lower.at[:, core, y]
-        for step in (1, 2, 3):
-            copies["spread", step] = start(
-                ref, ref, spread_send.at[step - 1], spread_recv.at[step - 1], along("y", step)
+        for way, step in ((0, 1), (1, 3)):
+            copies["spread", way] = start(ref, ref, spread_send.at[way], spread_recv.at[way], along("y", step))
+
+    def lower_relay():
+        for way, step in ((0, 1), (1, 3)):
+            copies["spread", way].wait_recv()
+            ref = column_lower.at[:, core, (y + 4 - step) % 4, :, pl.ds(way * HALF, HALF)]
+            copies["spread", 2 + way] = start(
+                ref, ref, spread_send.at[2 + way], spread_recv.at[2 + way], along("y", step)
             )
 
     def lower_both():
-        for step in (1, 2, 3):
-            copies["spread", step].wait_recv()
+        for way in range(2):
+            copies["spread", 2 + way].wait_recv()
         ref = column_lower.at[:, core]
         copies["both"] = start(ref, ref, both_sem.at[0], both_sem.at[1], partner)
 
@@ -373,15 +391,15 @@
                 block = first_block(node) + earlier
                 blocks_out[block, core, half, y, x, z] = tail[block, :, lanes] + total[earlier]
 
-    orders = ("zxy", "yzx", "xyz")
+    orders = ("yxz", "yzx", "yxz", "zxy", "yzx", "xyz")
 
     def up_ref(block, level, **other):
-        done = orders[block % 3][:level]
+        done = orders[block][:level]
         where = [other.get(a, slice(None) if a in done else coordinate[a]) for a in "yxz"]
         return blocks_out.at[(block, core, slice(None), *where)]
 
     def up_start(block, level):
-        axis = orders[block % 3][level]
+        axis = orders[block][level]
         ref = up_ref(block, level)
         for step in (1, 2, 3):
             sems = (block, level, step - 1)
@@ -392,7 +410,7 @@
             copies["up", block, level, step].wait_recv()
 
     def pair_start(block, step):
-        axis = orders[block % 3][2]
+        axis = orders[block][2]
         ref = up_ref(block, 2, **{axis: (coordinate[axis] - step) % 4})
         copies["pair", block, step] = start(ref, ref, pair_send.at[block, step], pair_recv.at[block, step], partner)
 
@@ -469,19 +487,23 @@
     multiply(0)
     second_forward(1)
     second_phase(2)
+    lower_relay()
     reduce_start(0)
     chain(1, 0)
     multiply(1)
     second_forward(2)
+    reduce_relay(0)
+    reduce_start(1)
     lower_both()
-    reduce_start(1)
     chain(2, 0)
     chain(2, 1)
+    reduce_relay(1)
     finish(0)
     rows_start(0)
     multiply(2)
+    reduce_start(2)
     prepare_tilde()
-    reduce_start(2)
+    reduce_relay(2)
     inner_products(0)
     down_start(0, 0)
     finish(1)
@@ -554,7 +576,9 @@
             pltpu.VMEM((NODES, 4, 2, PIECE, SN), F32),
             pltpu.VMEM((NODES, 4, PIECE, SN), F32),
             pltpu.VMEM((NODES, 4, PIECE, SN), F32),
-            pltpu.VMEM((NODES, 3, 4, PIECE, QUARTER), F32),
+            pltpu.VMEM((NODES, 2, 2, PIECE, QUARTER), F32),
+            pltpu.VMEM((NODES, 2, 4, PIECE, QUARTER), F32),
+            pltpu.VMEM((NODES, 2, 4, PIECE, QUARTER), F32),
             pltpu.VMEM((NODES, 4, 2, PIECE, QUARTER), F32),
             pltpu.VMEM((3,) + square, F32),
             pltpu.VMEM((3,) + square, BF16),
@@ -575,13 +599,13 @@
             dma((NODES, 2, 8)),
             dma((NODES, 2, 8)),
             dma((2,)),
-            dma((3,)),
-            dma((3,)),
+            dma((4,)),
+            dma((4,)),
             dma((2,)),
             dma((NODES, 2)),
             dma((NODES, 2)),
-            dma((NODES, 3)),
-            dma((NODES, 3)),
+            dma((NODES, 4)),
+            dma((NODES, 4)),
             dma((NODES, 3)),
             dma((NODES, 3)),
             dma((NODES, 2)),
@@ -599,32 +623,53 @@
     )(ancestor_inverse, factor, coupling, diagonal_inverse, ancestors)
 
 
-def assemble_kernel(blocks, rows, columns, out, rows_out, columns_out):
-    first, second = pl.program_id(0), pl.program_id(1)
-    later, earlier = jnp.maximum(first, second), jnp.minimum(first, second)
-    block = later * (later + 1) // 2 + earlier
+def block_at(step):
+    return jnp.where(step > 1, step - 1, step) - jnp.where(step > 4, 1, 0) - jnp.where(step > 6, 1, 0)
+
+
+def place_at(step):
+    turned = jnp.logical_or(step == 2, jnp.logical_or(step == 5, step == 7))
+    later = jnp.where(step > 3, 2, jnp.where(step > 0, 1, 0))
+    earlier = jnp.where(step == 8, 2, jnp.where(jnp.logical_or(step == 3, step // 2 == 3), 1, 0))
+    return turned, jnp.where(turned, earlier, later), jnp.where(turned, later, earlier)
+
+
+def assemble_kernel(block, rows, columns, out, rows_out, columns_out, sems):
+    step = pl.program_id(0)
+    turned = place_at(step)[0]
+
+    def copies():
+        return (
+            pltpu.make_async_copy(rows, rows_out, sems.at[0]),
+            pltpu.make_async_copy(columns, columns_out, sems.at[1]),
+        )
 
     def lanes(half):
-        return blocks[block, half // 2, half % 2].reshape(SN, QUARTER)
-
-    @pl.when(jnp.logical_and(first == 0, second == 0))
+        return block[0, half // 2, half % 2].reshape(SN, QUARTER)
+
+    @pl.when(step == 0)
     def _():
-        rows_out[...] = rows[...]
-        columns_out[...] = columns[...]
-
-    @pl.when(first >= second)
+        for copy in copies():
+            copy.start()
+
+    @pl.when(jnp.logical_not(turned))
     def _():
         for half in range(4):
             out[0, 0, :, half * QUARTER : (half + 1) * QUARTER] = lanes(half)
 
-    @pl.when(first < second)
+    @pl.when(turned)
     def _():
         for half in range(4):
             out[0, 0, half * QUARTER : (half + 1) * QUARTER, :] = lanes(half).T
 
+    @pl.when(step == 8)
+    def _():
+        for copy in copies():
+            copy.wait()
+
 
 def assemble(blocks, rows, columns):
-    whole = pl.BlockSpec(memory_space=pltpu.VMEM)
+    hbm = pl.BlockSpec(memory_space=pl.ANY)
     return pl.pallas_call(
         assemble_kernel,
         out_shape=(
@@ -632,14 +677,15 @@
             jax.ShapeDtypeStruct(rows.shape, F32),
             jax.ShapeDtypeStruct(columns.shape, F32),
         ),
-        grid=(NODES, NODES),
-        in_specs=[whole, whole, whole],
+        grid=(9,),
+        in_specs=[
+            pl.BlockSpec((1, 2, 2, 4, 4, 4, 8, QUARTER), lambda step: (block_at(step),) + (0,) * 7), hbm, hbm
+        ],
         out_specs=(
-            pl.BlockSpec((1, 1, SN, SN), lambda first, second: (first, second, 0, 0)),
-            pl.BlockSpec(rows.shape, lambda first, second: (0, 0, 0)),
-            pl.BlockSpec(columns.shape, lambda first, second: (0, 0, 0)),
+            pl.BlockSpec((1, 1, SN, SN), lambda step: place_at(step)[1:] + (0, 0)), hbm, hbm
         ),
-        compiler_params=pltpu.CompilerParams(vmem_limit_bytes=24 << 20),
+        scratch_shapes=[pltpu.SemaphoreType.DMA((2,))],
+        compiler_params=pltpu.CompilerParams(vmem_limit_bytes=60 << 20),
         name="assemble_node_blocks",
     )(blocks, rows, columns)
 

time: 150 us -> 182 us (1.21)
  Pallas kernels: 144 us -> 181 us
  local copies, waits for them, and re-layouts: 4.91 us -> 0 us
    pallas_call x1, Pallas kernels: 6.16 us -> 39.1 us  [assemble(): pl.pallas_call(assemble_kernel, out_shape=(jax.ShapeDtypeStruct((NODES, N...]
    unnamed x6 -> x0, local copies, waits for them, and re-layouts: 4.91 us -> none
    pallas_call x1, Pallas kernels: 138 us -> 142 us  [fused(): pl.pallas_call(kernel, out_shape=(jax.ShapeDtypeStruct((NODES, PIECE, SN)...]
where the time goes in v4:
time: 182 us
  Pallas kernels  181 us (99%)
    pallas_call x1, Pallas kernels, fused(): pl.pallas_call(kernel, out_shape=(jax.ShapeDtypeStruct((NODES, PIECE, SN)...  142 us
    pallas_call x1, Pallas kernels, assemble(): pl.pallas_call(assemble_kernel, out_shape=(jax.ShapeDtypeStruct((NODES, N...  39.1 us

profile of v4, /device:TPU:1, one launch (start us, length us, event | category | flops | bytes accessed | tf_op | source)
XLA Modules:
  0.0 181.7 jit_solution(1812763168776360267)
XLA Ops:
  0.6 141.8 %selected_inversion.1 = (f32[3,96,512]{2,1,0:T(8,128)}, f32[3,96,512]{2,1,0:T(8,128)}, f32[6,2,2,4,4,4,8,128]{7,6,5,4,3,2,1,0:T(8,128)}) custom-call(f32[1536,768]{1,0:T(8,128)} %inverse.1, bf16[3,96,512]{2,1,0:T(8,128)(2,1)} %factor.1, f32[3,512,512]{2,1,0:T(8,128)} %coupling.1, f32[3,512,512]{2,1,0:T(8,128)} %diagonal.1, s32[3,24]{1,0:T(4,128)} %ancestors.1), custom_call_target="tpu_custom_call" | custom-call | tf_op jit(solution)/shard_map/selected_inversion/pallas_call | solution.py:561
  142.4 39.1 %assemble_node_blocks.1 = (f32[3,3,512,512]{3,2,1,0:T(8,128)}, f32[3,96,512]{2,1,0:T(8,128)}, f32[3,96,512]{2,1,0:T(8,128)}) custom-call(f32[6,2,2,4,4,4,8,128]{7,6,5,4,3,2,1,0:T(8,128)} %get-tuple-element.9.block, f32[3,96,512]{2,1,0:T(8,128)} %get-tuple-element.10.rows, f32[3,96,512]{2,1,0:T(8,128)} %get-tuple-element.11.columns), custom_call_target="tpu_custom_call" | custom-call | tf_op jit(solution)/shard_map/assemble_node_blocks/pallas_call | solution.py:673

commit v5 on v4

--- a/solution.py
+++ b/solution.py
@@ -464,11 +464,11 @@
 
     for node in range(NODES):
         first_phase(node)
-    lower_start()
     first_forward(0)
     second_phase(0)
     first_forward(1)
     first_forward(2)
+    lower_start()
     load_inv.wait()
     for block in range(6):
         where = slice(block * 256, (block + 1) * 256)
@@ -490,6 +490,7 @@
     lower_relay()
     reduce_start(0)
     chain(1, 0)
+    tail_terms()
     multiply(1)
     second_forward(2)
     reduce_relay(0)
@@ -503,38 +504,37 @@
     multiply(2)
     reduce_start(2)
     prepare_tilde()
+    inner_products(0)
     reduce_relay(2)
-    inner_products(0)
+    columns_start(0)
     down_start(0, 0)
     finish(1)
     rows_start(1)
     inner_products(1)
     down_start(1, 0)
-    columns_start(0)
-    tail_terms()
     down_middle(0)
     down_middle(1)
+    finish(2)
+    rows_start(2)
+    inner_products(2)
+    down_start(2, 0)
     columns_start(1)
     down_last(0)
     down_last(1)
     for block in (0, 1, 2):
         up_start(block, 0)
-    finish(2)
-    rows_start(2)
-    inner_products(2)
-    down_start(2, 0)
+    down_middle(2)
+    columns_start(2)
     for block in (0, 1, 2):
         up_wait(block, 0)
         up_start(block, 1)
-    down_middle(2)
-    columns_start(2)
+    down_last(2)
+    for block in (3, 4, 5):
+        up_start(block, 0)
     for block in (0, 1, 2):
         up_wait(block, 1)
         up_start(block, 2)
         pair_start(block, 0)
-    down_last(2)
-    for block in (3, 4, 5):
-        up_start(block, 0)
     for block in (3, 4, 5):
         up_wait(block, 0)
         up_start(block, 1)
@@ -634,23 +634,17 @@
     return turned, jnp.where(turned, earlier, later), jnp.where(turned, later, earlier)
 
 
-def assemble_kernel(block, rows, columns, out, rows_out, columns_out, sems):
+def assemble_kernel(block, rows, columns, out, rows_out, columns_out):
     step = pl.program_id(0)
     turned = place_at(step)[0]
 
-    def copies():
-        return (
-            pltpu.make_async_copy(rows, rows_out, sems.at[0]),
-            pltpu.make_async_copy(columns, columns_out, sems.at[1]),
-        )
-
     def lanes(half):
         return block[0, half // 2, half % 2].reshape(SN, QUARTER)
 
     @pl.when(step == 0)
     def _():
-        for copy in copies():
-            copy.start()
+        rows_out[...] = rows[...]
+        columns_out[...] = columns[...]
 
     @pl.when(jnp.logical_not(turned))
     def _():
@@ -662,14 +656,9 @@
         for half in range(4):
             out[0, 0, half * QUARTER : (half + 1) * QUARTER, :] = lanes(half).T
 
-    @pl.when(step == 8)
-    def _():
-        for copy in copies():
-            copy.wait()
-
 
 def assemble(blocks, rows, columns):
-    hbm = pl.BlockSpec(memory_space=pl.ANY)
+    whole = pl.BlockSpec(rows.shape, lambda step: (0, 0, 0))
     return pl.pallas_call(
         assemble_kernel,
         out_shape=(
@@ -679,12 +668,11 @@
         ),
         grid=(9,),
         in_specs=[
-            pl.BlockSpec((1, 2, 2, 4, 4, 4, 8, QUARTER), lambda step: (block_at(step),) + (0,) * 7), hbm, hbm
+            pl.BlockSpec((1, 2, 2, 4, 4, 4, 8, QUARTER), lambda step: (block_at(step),) + (0,) * 7), whole, whole
         ],
         out_specs=(
-            pl.BlockSpec((1, 1, SN, SN), lambda step: place_at(step)[1:] + (0, 0)), hbm, hbm
+            pl.BlockSpec((1, 1, SN, SN), lambda step: place_at(step)[1:] + (0, 0)), whole, whole
         ),
-        scratch_shapes=[pltpu.SemaphoreType.DMA((2,))],
         compiler_params=pltpu.CompilerParams(vmem_limit_bytes=60 << 20),
         name="assemble_node_blocks",
     )(blocks, rows, columns)

time: 182 us -> 152 us (0.84); the launches traced: 182 us -> 150 us
  Pallas kernels: 181 us -> 149 us
    pallas_call x1, Pallas kernels: 39.1 us -> 10.6 us  [assemble(): pl.pallas_call(assemble_kernel, out_shape=(jax.ShapeDtypeStruct((NODES, N...]
    pallas_call x1, Pallas kernels: 142 us -> 139 us  [fused(): pl.pallas_call(kernel, out_shape=(jax.ShapeDtypeStruct((NODES, PIECE, SN)...]
where the time goes in v5:
time: 152 us; the launch traced here: 150 us
  Pallas kernels  149 us (98%)
    pallas_call x1, Pallas kernels, fused(): pl.pallas_call(kernel, out_shape=(jax.ShapeDtypeStruct((NODES, PIECE, SN)...  139 us
    pallas_call x1, Pallas kernels, assemble(): pl.pallas_call(assemble_kernel, out_shape=(jax.ShapeDtypeStruct((NODES, N...  10.6 us

profile of v5, /device:TPU:1, one launch (start us, length us, event | category | flops | bytes accessed | tf_op | source)
XLA Modules:
  0.0 149.8 jit_solution(442384300182158014)
XLA Ops:
  0.6 138.5 %selected_inversion.1 = (f32[3,96,512]{2,1,0:T(8,128)}, f32[3,96,512]{2,1,0:T(8,128)}, f32[6,2,2,4,4,4,8,128]{7,6,5,4,3,2,1,0:T(8,128)}) custom-call(f32[1536,768]{1,0:T(8,128)} %inverse.1, bf16[3,96,512]{2,1,0:T(8,128)(2,1)} %factor.1, f32[3,512,512]{2,1,0:T(8,128)} %coupling.1, f32[3,512,512]{2,1,0:T(8,128)} %diagonal.1, s32[3,24]{1,0:T(4,128)} %ancestors.1), custom_call_target="tpu_custom_call" | custom-call | tf_op jit(solution)/shard_map/selected_inversion/pallas_call | solution.py:561
  139.1 10.6 %assemble_node_blocks.1 = (f32[3,3,512,512]{3,2,1,0:T(8,128)}, f32[3,96,512]{2,1,0:T(8,128)}, f32[3,96,512]{2,1,0:T(8,128)}) custom-call(f32[6,2,2,4,4,4,8,128]{7,6,5,4,3,2,1,0:T(8,128)} %get-tuple-element.9.block, f32[3,96,512]{2,1,0:T(8,128)} %get-tuple-element.10.rows, f32[3,96,512]{2,1,0:T(8,128)} %get-tuple-element.11.columns), custom_call_target="tpu_custom_call" | custom-call | tf_op jit(solution)/shard_map/assemble_node_blocks/pallas_call | solution.py:662
